TPU v7x, 1024 devices: a whole 4x8x16 slice. The times are simulated.
1024 devices in a mesh: pipe: 16 (over y, core), expert: 64 (over x, z).
Axes of the slice: x: 4, y: 8, z: 16, core: 2. Of those that a mesh axis runs over, the one named last changes fastest.
Arguments:
- grad_sent: bfloat16 [16, 8192, 2048], P('pipe', 'expert'), may hold values from -6 to 6
- routes: int32 [16, 8192, 2], P('pipe', 'expert'), may hold values from 0 to 63, all different within a row; in each aligned block of 64 rows (0 to 63, 64 to 127, ..., all dimensions but the last counted through in order) at most 3 rows name the same one
- router_probs: float32 [16, 8192, 64], P('pipe', 'expert'), may hold values from 0.003125 to 0.078125
- saved_hidden: bfloat16 [16, 24576, 768], P('pipe', 'expert'), may hold values from -6 to 6
- w_down: bfloat16 [64, 768, 2048], P('expert'), may hold values from -0.21875 to 0.21875
- w_router: bfloat16 [2048, 64], replicated, may hold values from -0.125 to 0.125
Outputs:
- d_hidden: bfloat16 [16, 24576, 768], P('pipe', 'expert')
- grad_router_in: bfloat16 [16, 8192, 2048], P('pipe', 'expert')
Inputs may be any that keep to these rules, and one draw needn't show every extreme that they name: `routes`: each token names 2 different experts. In each micro-batch of one device (an aligned block of 64 rows) no expert is named by more than 3 tokens, a bound that some block reaches.
All inputs are finite; a program needn't handle non-finite values.
Results may differ from a plain program's by a relative error of at most 0.0046.
Values may be sent and summed in bfloat16 or wider, within the bound.
A program may use at most 32 MiB of HBM per device.

v0:
```python
import jax
import jax.numpy as jnp
from jax import lax
from jax.sharding import PartitionSpec as P

TOP = 2
MICRO = 2
MB_TOK = 64


def from_behind(block, axis, distance):
    devices = range(lax.axis_size(axis))
    route = [((i - distance) % len(devices), i) for i in devices]
    return lax.ppermute(block, axis, route)


def route_slots(route_rows, peer_count, capacity):
    onehot = (route_rows[..., None] == jnp.arange(peer_count, dtype=jnp.int32)).astype(jnp.int32)
    rank_of = jnp.sum((jnp.cumsum(onehot, axis=1) - onehot) * onehot, axis=2)
    return route_rows * capacity + rank_of


def on_device(grad_sent, routes, router_probs, saved_hidden, w_down, w_router):
    peer_count = lax.axis_size("expert")
    slot_count = saved_hidden.shape[1]
    capacity = slot_count // (MICRO * peer_count)
    send_width = peer_count * capacity
    model_width = grad_sent.shape[2]
    hidden_width = saved_hidden.shape[2]
    tokens = routes.shape[1]
    incoming = from_behind(grad_sent, "pipe", -1)[0]
    route_rows = routes[0].reshape(MICRO, MB_TOK * TOP)
    position = route_slots(route_rows, peer_count, capacity)
    chosen = jnp.take_along_axis(router_probs[0], routes[0], axis=1)
    weights = chosen / jnp.sum(chosen, axis=1, keepdims=True)
    rounded = weights.astype(jnp.bfloat16)
    micro_index = jnp.arange(MICRO, dtype=jnp.int32)[:, None]
    token_index = jnp.broadcast_to(
        jnp.arange(MB_TOK * TOP, dtype=jnp.int32)[None, :] // TOP, (MICRO, MB_TOK * TOP)
    )
    slot_token = (
        jnp.zeros((MICRO, send_width), jnp.int32).at[micro_index, position].set(token_index)
    )
    slot_used = jnp.zeros((MICRO, send_width), jnp.bool_).at[micro_index, position].set(True)
    send_scale = (
        jnp.zeros((MICRO, send_width), jnp.bfloat16)
        .at[micro_index, position]
        .set(rounded.reshape(MICRO, MB_TOK * TOP))
    )
    micro_grad = incoming.reshape(MICRO, MB_TOK, model_width)
    picked = jnp.take_along_axis(micro_grad, slot_token[..., None], axis=1)
    send_rows = jnp.where(slot_used[..., None], picked, jnp.zeros((), jnp.bfloat16))
    hidden = saved_hidden[0].reshape(MICRO, send_width, hidden_width)
    weight = w_down[0]
    arrived, arrived_scale = (
        lax.all_to_all(send_rows, "expert", split_axis=1, concat_axis=1, tiled=True),
        lax.all_to_all(send_scale, "expert", split_axis=1, concat_axis=1, tiled=True),
    )
    flat_rows = arrived.reshape(-1, model_width)
    flat_saved = hidden.reshape(flat_rows.shape[0], hidden_width)
    grad_hidden = lax.dot_general(
        flat_rows, weight, (((1,), (1,)), ((), ())), preferred_element_type=jnp.float32
    )
    route_grad = jnp.sum(grad_hidden * flat_saved.astype(jnp.float32), axis=1)
    scaled = (arrived_scale.reshape(-1, 1).astype(jnp.float32) * grad_hidden).astype(jnp.bfloat16)
    d_hidden, route_grad = (scaled, route_grad.reshape(arrived_scale.shape))
    returned = lax.all_to_all(route_grad, "expert", split_axis=1, concat_axis=1, tiled=True)
    slot_grad = jnp.take_along_axis(returned, position, axis=1).reshape(tokens, TOP)
    centred = slot_grad - jnp.sum(weights * slot_grad, axis=1, keepdims=True)
    logit_part = weights * centred
    onehot_tok = (routes[0][..., None] == jnp.arange(peer_count, dtype=jnp.int32)).astype(
        jnp.float32
    )
    logit_grad = jnp.sum(logit_part[..., None] * onehot_tok, axis=1)
    grad_in = jnp.dot(logit_grad, w_router.astype(jnp.float32).T, precision=lax.Precision.HIGHEST)
    return (d_hidden.reshape(1, slot_count, hidden_width), grad_in.astype(jnp.bfloat16)[None])


def solution(mesh):
    placed = (
        P("pipe", "expert", None),
        P("pipe", "expert", None),
        P("pipe", "expert", None),
        P("pipe", "expert", None),
        P("expert", None, None),
        P(),
    )
    return jax.shard_map(
        on_device,
        mesh=mesh,
        in_specs=placed,
        out_specs=(P("pipe", "expert", None), P("pipe", "expert", None)),
        check_vma=False,
    )
```

profile of v0, /device:TPU:1, one launch (start us, length us, event | category | flops | bytes accessed | tf_op | source)
XLA Modules:
  0.0 211.6 jit_solution(13016243878084654212)
XLA Ops:
  0.7 14.2 %collective-permute-start = (bf16[1,128,2048]{2,1,0:T(8,128)(2,1)}, bf16[1,128,2048]{2,1,0:T(8,128)(2,1)}, u32[]{:S(2)}, u32[]{:S(2)}) collective-permute-start(bf16[1,128,2048]{2,1,0:T(8,128)(2,1)} %param.6), channel_id=1, source_target_pairs={{64,0},{128,64},{192,128},{256,192},{320,256},{384,320},{448,384},... | collective-permute-start | bytes 1572872 | tf_op jit(solution)/shard_map/ppermute | solution.py:14
  14.8 0.8 copy.52
  15.6 0.7 broadcast_multiply_fusion
  16.3 0.7 fusion.11
  17.0 0.1 eq.28
  17.1 0.1 fusion.5
  17.2 0.2 reduce_window_sum.11
  17.4 0.2 select_reduce_fusion
  17.6 0.1 copy.51
  17.7 0.1 mul.61
  17.9 0.1 copy.53
  18.0 0.1 reshape.232
  18.1 2.0 gather_fusion
  20.1 0.1 reshape.235
  20.4 0.1 div.27
  20.4 0.1 div.28
  20.5 0.1 div.29
  20.7 0.1 copy-done.4
  20.8 12.5 %scatter_fusion = bf16[2,192]{1,0:T(2,128)(2,1)S(1)} fusion(bf16[2,192]{1,0:T(2,128)(2,1)S(1)} %broadcast_in_dim.42, s32[256]{0:T(256)S(1)} %get-tuple-element.9, bf16[256]{0:T(256)(128)(2,1)S(1)} %fusion.14), kind=kCustom, calls=%fused_computation.3 | custom fusion | bytes 3584 | tf_op jit(solution)/shard_map/scatter | solution.py:48
  33.3 0.2 all_to_all.17
  33.5 0.7 copy.55
  34.1 9.4 %all-to-all-start = ((bf16[2,64,3]{2,0,1:T(2,128)(2,1)}), bf16[2,64,3]{2,0,1:T(2,128)(2,1)S(1)}, u32[]{:S(2)}, u32[]{:S(2)}) async-start(bf16[2,64,3]{2,0,1:T(2,128)(2,1)} %copy.55), calls=%async_computation | async-start | bytes 65536 | tf_op jit(solution)/shard_map/all_to_all | solution.py:57
  43.6 12.5 %scatter_fusion.2 = s32[2,192]{1,0:T(2,128)S(1)} fusion(s32[2,192]{1,0:T(2,128)S(1)} %broadcast_in_dim.78, s32[256]{0:T(256)S(1)} %get-tuple-element.9, s32[256]{0:T(256)S(1)} %broadcast_bitcast_fusion), kind=kCustom, calls=%fused_computation.5 | custom fusion | bytes 5120 | tf_op jit(solution)/shard_map/scatter | solution.py:42
  56.1 0.1 reshape.238
  56.2 0.2 copy.59
  56.4 12.6 %scatter_fusion.1 = pred[2,192]{1,0:T(4,128)(4,1)S(1)} fusion(pred[2,192]{1,0:T(4,128)(4,1)S(1)} %broadcast_in_dim.75, s32[256]{0:T(256)S(1)} %get-tuple-element.9, pred[256]{0:T(512)(128)(4,1)S(1)} %broadcast.292), kind=kCustom, calls=%fused_computation.4 | custom fusion | bytes 2816 | tf_op jit(solution)/shard_map/scatter | solution.py:44
  69.0 0.2 copy.58
  69.1 15.7 %gather_fusion.1 = bf16[384,2048]{1,0:T(8,128)(2,1)} fusion(bf16[2,64,2048]{2,1,0:T(8,128)(2,1)} %bitcast.8, s32[384]{0:T(512)S(1)} %reshape.238), kind=kCustom, calls=%fused_computation.1 | custom fusion | bytes 3148800 | tf_op jit(solution)/shard_map/jit(take_along_axis)/gather | solution.py:51
  84.8 5.1 %broadcast_select_fusion.1 = bf16[2,192,2048]{2,0,1:T(2,128)(2,1)} fusion(pred[2,192]{0,1:T(8,128)(4,1)S(1)} %copy.58, pred[2,192]{0,1:T(8,128)(4,1)S(1)} %copy.59, bf16[2,192,2048]{2,1,0:T(8,128)(2,1)} %bitcast.55), kind=kLoop, calls=%fused_computation.9 | loop fusion | flops 1572864 | bytes 3146496 | tf_op jit(solution)/shard_map/jit(_where)/select_n | solution.py:52
  89.9 14.9 %all-to-all-start.1 = ((bf16[2,192,2048]{2,0,1:T(2,128)(2,1)}), bf16[2,192,2048]{2,0,1:T(2,128)(2,1)}, u32[]{:S(2)}, u32[]{:S(2)}) async-start(bf16[2,192,2048]{2,0,1:T(2,128)(2,1)} %broadcast_select_fusion.1), calls=%async_computation.1 | async-start | bytes 3145728 | tf_op jit(solution)/shard_map/all_to_all | solution.py:56
  104.9 0.1 copy.56
  105.0 0.1 copy.57
  105.1 0.2 reshape.230
  105.3 69.4 %all-to-all-done.1 = bf16[2,192,2048]{2,0,1:T(2,128)(2,1)} async-done(((bf16[2,192,2048]{2,0,1:T(2,128)(2,1)}), bf16[2,192,2048]{2,0,1:T(2,128)(2,1)}, u32[]{:S(2)}, u32[]{:S(2)}) %all-to-all-start.1) | async-done | bytes 1572896 | tf_op jit(solution)/shard_map/all_to_all | solution.py:56
  174.7 2.1 copy.61
  176.8 2.4 %fusion.3 = (f32[384]{0:T(512)S(1)}, bf16[1,384,768]{2,1,0:T(8,128)(2,1)}) fusion(bf16[1,384,768]{2,1,0:T(8,128)(2,1)S(1)} %copy-done.5, f32[384]{0:T(512)S(1)} %reshape.230, bf16[384,2048]{1,0:T(8,128)(2,1)S(1)} %bitcast.56, bf16[1,768,2048]{2,1,0:T(8,128)(2,1)S(1)} %copy-done), kind=kOutput, calls=%fused_computation.13 | convolution fusion | flops 1209433728 | bytes 5901312 | tf_op jit(solution)/shard_map/dot_general | solution.py:61
  179.1 0.2 all_to_all.20
  179.3 0.7 copy.63
  180.0 12.5 %all-to-all-start.2 = ((f32[2,64,3]{2,0,1:T(2,128)}), f32[2,64,3]{2,0,1:T(2,128)S(1)}, u32[]{:S(2)}, u32[]{:S(2)}) async-start(f32[2,64,3]{2,0,1:T(2,128)} %copy.63), calls=%async_computation.2 | async-start | bytes 131072 | tf_op jit(solution)/shard_map/all_to_all | solution.py:67
  192.5 0.1 reduce_sum.52
  192.7 0.7 copy.62
  193.3 12.7 %all-to-all-done.2 = f32[2,64,3]{2,0,1:T(2,128)S(1)} async-done(((f32[2,64,3]{2,0,1:T(2,128)}), f32[2,64,3]{2,0,1:T(2,128)S(1)}, u32[]{:S(2)}, u32[]{:S(2)}) %all-to-all-start.2) | async-done | bytes 1568 | tf_op jit(solution)/shard_map/all_to_all | solution.py:67
  206.0 0.1 all_to_all.22
  206.2 2.5 %gather_fusion.2 = f32[256]{0:T(256)S(1)} fusion(f32[2,192]{1,0:T(2,128)S(1)} %all_to_all.22, s32[256]{0:T(256)S(1)} %get-tuple-element.8), kind=kCustom, calls=%fused_computation.2 | custom fusion | bytes 4096 | tf_op jit(solution)/shard_map/jit(take_along_axis)/gather | solution.py:68
  208.7 0.1 gather.20
  208.9 0.7 multiply_reduce_fusion
  209.6 0.6 subtract_multiply_fusion
  210.2 1.4 fusion.2
  (28 shorter events, 0.3 us)
Async XLA Ops:
  0.6 176.1 %copy-start = (bf16[1,768,2048]{2,1,0:T(8,128)(2,1)S(1)}, bf16[1,768,2048]{2,1,0:T(8,128)(2,1)}, u32[]{:S(2)}) copy-start(bf16[1,768,2048]{2,1,0:T(8,128)(2,1)} %param.10) | copy-start | bytes 9437188
  0.6 17.5 %copy-start.1 = (f32[1,128,64]{1,2,0:T(8,128)S(1)}, f32[1,128,64]{1,2,0:T(8,128)}, u32[]{:S(2)}) copy-start(f32[1,128,64]{1,2,0:T(8,128)} %param.8) | copy-start | bytes 98308
  0.7 68.5 %collective-permute-start = (bf16[1,128,2048]{2,1,0:T(8,128)(2,1)}, bf16[1,128,2048]{2,1,0:T(8,128)(2,1)}, u32[]{:S(2)}, u32[]{:S(2)}) collective-permute-start(bf16[1,128,2048]{2,1,0:T(8,128)(2,1)} %param.6), channel_id=1, source_target_pairs={{64,0},{128,64},{192,128},{256,192},{320,256},{384,320},{448,384},... | collective-permute-start | bytes 1572872 | tf_op jit(solution)/shard_map/ppermute | solution.py:14
  18.1 2.2 %copy-start.3 = (s32[1,128,2]{1,2,0:T(2,128)S(1)}, s32[1,128,2]{1,2,0:T(2,128)}, u32[]{:S(2)}) copy-start(s32[1,128,2]{1,2,0:T(2,128)} %param.7) | copy-start | bytes 3076
  20.4 0.5 copy-start.4
  34.1 55.8 %all-to-all-start = ((bf16[2,64,3]{2,0,1:T(2,128)(2,1)}), bf16[2,64,3]{2,0,1:T(2,128)(2,1)S(1)}, u32[]{:S(2)}, u32[]{:S(2)}) async-start(bf16[2,64,3]{2,0,1:T(2,128)(2,1)} %copy.55), calls=%async_computation | async-start | bytes 65536 | tf_op jit(solution)/shard_map/all_to_all | solution.py:57
  89.9 84.7 %all-to-all-start.1 = ((bf16[2,192,2048]{2,0,1:T(2,128)(2,1)}), bf16[2,192,2048]{2,0,1:T(2,128)(2,1)}, u32[]{:S(2)}, u32[]{:S(2)}) async-start(bf16[2,192,2048]{2,0,1:T(2,128)(2,1)} %broadcast_select_fusion.1), calls=%async_computation.1 | async-start | bytes 3145728 | tf_op jit(solution)/shard_map/all_to_all | solution.py:56
  174.7 2.1 copy-start.5
  179.1 31.1 %copy-start.2 = (bf16[2048,64]{0,1:T(8,128)(2,1)S(1)}, bf16[2048,64]{0,1:T(8,128)(2,1)}, u32[]{:S(2)}) copy-start(bf16[2048,64]{0,1:T(8,128)(2,1)} %param.11) | copy-start | bytes 786436
  180.0 26.0 %all-to-all-start.2 = ((f32[2,64,3]{2,0,1:T(2,128)}), f32[2,64,3]{2,0,1:T(2,128)S(1)}, u32[]{:S(2)}, u32[]{:S(2)}) async-start(f32[2,64,3]{2,0,1:T(2,128)} %copy.63), calls=%async_computation.2 | async-start | bytes 131072 | tf_op jit(solution)/shard_map/all_to_all | solution.py:67
where the time goes:
time: 214 us; the launch traced here: 212 us
  waiting for transfers between devices  82.1 us (38%)
  local copies, waits for them, and re-layouts  65.5 us (31%)
  starting transfers between devices  51 us (24%)
  other arithmetic  8.36 us (4%)
  matrix products  3.77 us (2%)
    all_to_all x1, waiting for transfers between devices, on_device(): lax.all_to_all(send_rows, 'expert', split_axis=1, concat_axis=1, tiled=True)  69.4 us
    gather x2, local copies, waits for them, and re-layouts, on_device(): picked = jnp.take_along_axis(micro_grad, slot_token[..., None], axis=1)  15.8 us
    all_to_all x1, starting transfers between devices, on_device(): lax.all_to_all(send_rows, 'expert', split_axis=1, concat_axis=1, tiled=True)  14.9 us
    ppermute x1, starting transfers between devices, from_behind(): return lax.ppermute(block, axis, route)  14.2 us
    scatter x2, local copies, waits for them, and re-layouts, on_device(): jnp.zeros((MICRO, send_width), jnp.bool_).at[micro_index, position]  12.7 us
    all_to_all x1, waiting for transfers between devices, on_device(): lax.all_to_all(route_grad, 'expert', split_axis=1, concat_axis=1, tiled=T...  12.7 us
    scatter x1, local copies, waits for them, and re-layouts, on_device(): send_scale = jnp.zeros((MICRO, send_width), jnp.bfloat16).at[micro_index,...  12.5 us
    scatter x1, local copies, waits for them, and re-layouts, on_device(): jnp.zeros((MICRO, send_width), jnp.int32).at[micro_index, position]  12.5 us
  transfers between devices with their start and end apart: 4, of which 2 were waited for; matrix products, arithmetic and copies ran while one was open for 31% of the time, Pallas kernels for 0%

commit v1 on v0

v1 whole, which is shorter than its diff:
```python
import functools

import jax
import jax.numpy as jnp
from jax import lax
from jax.experimental import pallas as pl
from jax.experimental.pallas import tpu as pltpu
from jax.sharding import PartitionSpec as P

TOP = 2
MICRO = 2
CAP = 3
LANES = 128
F32 = jnp.float32
BF16 = jnp.bfloat16


def iota(shape, axis):
    return lax.broadcasted_iota(jnp.int32, shape, axis)


def dot(a, b, dims=((1,), (0,)), precision=None):
    return lax.dot_general(
        a, b, (dims, ((), ())), precision=precision, preferred_element_type=F32
    )


def kernel(
    columns,
    depth,
    routes_ref,
    probs_ref,
    router_ref,
    grad_ref,
    saved_hbm,
    weight_hbm,
    hidden_ref,
    grad_in_ref,
    incoming,
    pick,
    swap,
    send,
    recv,
    saved,
    weight,
    scale_send,
    scale_recv,
    partial,
    back_send,
    back_recv,
    load_sem,
    pipe_send,
    pipe_recv,
    send_sem,
    recv_sem,
    scale_send_sem,
    scale_recv_sem,
    back_send_sem,
    back_recv_sem,
):
    experts = columns * depth
    slab = depth * CAP
    tokens = incoming.shape[1]
    groups = incoming.shape[2] // LANES
    unit = groups * CAP
    pipes = lax.axis_size("pipe")
    stage = lax.axis_index("pipe")
    me = lax.axis_index("expert")
    column, level = me // depth, me % depth

    barrier = pltpu.get_barrier_semaphore()

    def greet(step, carry):
        pl.semaphore_signal(barrier, inc=1, device_id={"expert": (me + step) % experts})
        return carry

    lax.fori_loop(1, experts, greet, 0)
    for distance in (1, pipes - 1):
        pl.semaphore_signal(barrier, inc=1, device_id={"pipe": (stage + distance) % pipes})

    load_weight = pltpu.make_async_copy(weight_hbm.at[0], weight, load_sem.at[0])
    load_saved = pltpu.make_async_copy(saved_hbm.at[0], saved, load_sem.at[1])
    load_weight.start()
    load_saved.start()

    all_tokens = MICRO * tokens
    expert_row = iota((experts, all_tokens), 0)
    named = [(expert_row == routes_ref[k : k + 1, :]).astype(F32) for k in range(TOP)]
    probs = probs_ref[...]
    chosen = [jnp.sum(named[k] * probs, axis=0, keepdims=True) for k in range(TOP)]
    total = chosen[0] + chosen[1]
    weights = [chosen[k] / total for k in range(TOP)]
    before, after = iota((all_tokens, all_tokens), 0), iota((all_tokens, all_tokens), 1)
    earlier = (before < after) & ((before >= tokens) == (after >= tokens))
    seen = dot((named[0] + named[1]).astype(BF16), earlier.astype(F32).astype(BF16))
    rank = [jnp.sum(named[k] * seen, axis=0, keepdims=True) for k in range(TOP)]
    micro = (iota((1, all_tokens), 1) >= tokens).astype(F32)
    lane_row = iota((LANES, all_tokens), 0).astype(F32)
    slot = [(lane_row == micro * CAP + rank[k]).astype(F32) for k in range(TOP)]
    scales = sum(
        dot(
            named[k].astype(BF16),
            (slot[k] * weights[k].astype(BF16).astype(F32)).astype(BF16),
            ((1,), (1,)),
        )
        for k in range(TOP)
    )
    scale_send[...] = scales.reshape(experts, 1, LANES)
    row = [routes_ref[k : k + 1, :].astype(F32) * CAP + rank[k] for k in range(TOP)]
    for m in range(MICRO):
        here = iota((experts * CAP, tokens), 0).astype(F32)
        part = [row[k][:, m * tokens : (m + 1) * tokens] for k in range(TOP)]
        pick[m] = ((here == part[0]) | (here == part[1])).astype(F32).astype(BF16)

    size = slab * groups
    index = iota((size, 1), 0)
    outer = lax.shift_right_logical(index * ((1 << 16) // unit + 1), 16)
    inner = index - outer * unit
    third = lax.shift_right_logical(inner * ((1 << 16) // CAP + 1), 16)
    target = third * unit + outer * CAP + (inner - third * CAP)
    swap[...] = (iota((size, size), 1) == target).astype(F32).astype(BF16)

    pl.semaphore_wait(barrier, experts - 1 + 2)

    def pipe_copy(m):
        return pltpu.make_async_remote_copy(
            src_ref=grad_ref.at[0, pl.ds(m * tokens, tokens)],
            dst_ref=incoming.at[m],
            send_sem=pipe_send.at[m],
            recv_sem=pipe_recv.at[m],
            device_id={"pipe": (stage + pipes - 1) % pipes},
        )

    for m in range(MICRO):
        pipe_copy(m).start()

    def scale_copy(peer):
        return pltpu.make_async_remote_copy(
            src_ref=scale_send.at[peer],
            dst_ref=scale_recv.at[me],
            send_sem=scale_send_sem,
            recv_sem=scale_recv_sem,
            device_id={"expert": peer},
        )

    def scale_out(step, carry):
        scale_copy((me + step) % experts).start()
        return carry

    lax.fori_loop(1, experts, scale_out, 0)
    pltpu.make_async_copy(scale_send.at[me], scale_recv.at[me], scale_recv_sem).start()

    def row_copy(m, far, to):
        return pltpu.make_async_remote_copy(
            src_ref=send.at[m, far, to],
            dst_ref=recv.at[m, column, level],
            send_sem=send_sem.at[m, far],
            recv_sem=recv_sem.at[m, column],
            device_id={"expert": far * depth + to},
        )

    def hop(step):
        half = step // 2
        forward = depth // 2 - half
        backward = 2 * depth - (depth // 2 - 1 - half)
        return (level + jnp.where(step % 2 == 0, forward, backward)) % depth

    def fill(m, far):
        start = pl.multiple_of(far * slab, 16)
        rows = dot(pick[m, pl.ds(start, slab), :], incoming[m]).astype(BF16)
        stacked = jnp.concatenate(
            [rows[:, j * LANES : (j + 1) * LANES] for j in range(groups)], axis=0
        )
        mixed = dot(swap[...], stacked).astype(BF16)
        send[m, far] = mixed.reshape(depth, unit, LANES)

    for m in range(MICRO):
        pipe_copy(m).wait_recv()

        def spread(turn, carry):
            far = (column + turn) % columns
            fill(m, far)

            def out(step, inner_carry):
                row_copy(m, far, hop(step)).start()
                return inner_carry

            lax.fori_loop(0, jnp.where(turn == 0, depth - 1, depth), out, 0)
            return carry

        lax.fori_loop(0, columns, spread, 0)
        pltpu.make_async_copy(
            send.at[m, column, level], recv.at[m, column, level], recv_sem.at[m, column]
        ).start()

    load_weight.wait()
    load_saved.wait()
    pltpu.make_async_copy(scale_send, scale_recv, scale_recv_sem).wait()

    owner = iota((slab, depth), 0)
    holder = (
        lax.shift_right_logical(owner * ((1 << 16) // CAP + 1), 16) == iota((slab, depth), 1)
    ).astype(F32)
    line = iota((slab, LANES), 0)
    own_rank = line - lax.shift_right_logical(line * ((1 << 16) // CAP + 1), 16) * CAP
    holder_t = (
        iota((depth, slab), 0)
        == lax.shift_right_logical(iota((depth, slab), 1) * ((1 << 16) // CAP + 1), 16)
    ).astype(F32)

    def back_copy(peer):
        return pltpu.make_async_remote_copy(
            src_ref=back_send.at[peer],
            dst_ref=back_recv.at[me],
            send_sem=back_send_sem,
            recv_sem=back_recv_sem,
            device_id={"expert": peer},
        )

    for m in range(MICRO):
        ours = iota((slab, LANES), 1) == own_rank + m * CAP

        def gather(turn, carry):
            source = (column + columns - turn) % columns
            pltpu.make_async_copy(
                send.at[m, source], recv.at[m, source], recv_sem.at[m, source]
            ).wait()
            mixed = recv[m, source].reshape(size, LANES)
            rows = dot(swap[...], mixed).astype(BF16)
            flat = jnp.concatenate(
                [rows[j * slab : (j + 1) * slab] for j in range(groups)], axis=1
            )
            grad = dot(flat, weight[...], ((1,), (1,)))
            start = pl.multiple_of((m * columns + source) * slab, 16)
            held = saved[pl.ds(start, slab), :].astype(F32)
            route_grad = jnp.sum(grad * held, axis=1, keepdims=True)
            first = pl.multiple_of(source * depth, 16)
            all_scales = scale_recv[pl.ds(first, depth)].reshape(depth, LANES)
            spread_scales = dot(holder.astype(BF16), all_scales.astype(BF16))
            scale = jnp.sum(jnp.where(ours, spread_scales, 0.0), axis=1, keepdims=True)
            hidden_ref[0, pl.ds(start, slab), :] = (scale * grad).astype(BF16)
            sums = dot(
                holder_t, jnp.where(ours, route_grad, 0.0), precision=lax.Precision.HIGHEST
            )
            if m == 0:
                partial[pl.ds(first, depth), :] = sums
            else:
                both = partial[pl.ds(first, depth), :] + sums
                back_send[pl.ds(first, depth)] = both.reshape(depth, 1, LANES)

                def back(step, inner_carry):
                    back_copy(source * depth + hop(step)).start()
                    return inner_carry

                lax.fori_loop(0, jnp.where(turn == 0, depth - 1, depth), back, 0)
            return carry

        lax.fori_loop(0, columns, gather, 0)
    pltpu.make_async_copy(back_send.at[me], back_recv.at[me], back_recv_sem).start()

    for m in range(MICRO):
        pipe_copy(m).wait_send()

        def left(turn, carry):
            far = (column + turn) % columns
            pltpu.make_async_copy(send.at[m, far], recv.at[m, far], send_sem.at[m, far]).wait()
            return carry

        lax.fori_loop(1, columns, left, 0)
        pltpu.make_async_copy(
            send.at[m, column, pl.ds(0, depth - 1)],
            recv.at[m, column, pl.ds(0, depth - 1)],
            send_sem.at[m, column],
        ).wait()
    others = pl.ds(0, experts - 1)
    pltpu.make_async_copy(scale_send.at[others], scale_recv.at[others], scale_send_sem).wait()

    pltpu.make_async_copy(back_send, back_recv, back_recv_sem).wait()
    returned = back_recv[...].reshape(experts, LANES)
    slot_grad = [
        jnp.sum(
            slot[k] * dot(returned, named[k], ((0,), (0,)), lax.Precision.HIGHEST),
            axis=0,
            keepdims=True,
        )
        for k in range(TOP)
    ]
    mean = weights[0] * slot_grad[0] + weights[1] * slot_grad[1]
    logit = sum(named[k] * (weights[k] * (slot_grad[k] - mean)) for k in range(TOP))
    logit = logit.T
    high = logit.astype(BF16)
    low = (logit - high.astype(F32)).astype(BF16)
    router = router_ref[...]
    grad_in_ref[0] = (dot(high, router) + dot(low, router)).astype(BF16)
    pltpu.make_async_copy(back_send.at[others], back_recv.at[others], back_send_sem).wait()


def solution(mesh):
    experts = mesh.shape["expert"]

    def on_device(grad_sent, routes, router_probs, saved_hidden, w_down, w_router):
        model_width = grad_sent.shape[2]
        slots, width = saved_hidden.shape[1:]
        tokens = routes.shape[1] // MICRO
        depth = model_width // LANES
        columns = experts // depth
        slab = depth * CAP
        unit = depth * CAP
        in_vmem = pl.BlockSpec(memory_space=pltpu.VMEM)
        in_place = pl.BlockSpec(memory_space=pl.ANY)
        return pl.pallas_call(
            functools.partial(kernel, columns, depth),
            out_shape=(
                jax.ShapeDtypeStruct((1, slots, width), BF16),
                jax.ShapeDtypeStruct((1, MICRO * tokens, model_width), BF16),
            ),
            in_specs=[in_vmem, in_vmem, in_vmem, in_place, in_place, in_place],
            out_specs=(in_vmem, in_vmem),
            scratch_shapes=[
                pltpu.VMEM((MICRO, tokens, model_width), BF16),
                pltpu.VMEM((MICRO, experts * CAP, tokens), BF16),
                pltpu.VMEM((slab * depth, slab * depth), BF16),
                pltpu.VMEM((MICRO, columns, depth, unit, LANES), BF16),
                pltpu.VMEM((MICRO, columns, depth, unit, LANES), BF16),
                pltpu.VMEM((slots, width), BF16),
                pltpu.VMEM((width, model_width), BF16),
                pltpu.VMEM((experts, 1, LANES), F32),
                pltpu.VMEM((experts, 1, LANES), F32),
                pltpu.VMEM((experts, LANES), F32),
                pltpu.VMEM((experts, 1, LANES), F32),
                pltpu.VMEM((experts, 1, LANES), F32),
                pltpu.SemaphoreType.DMA((2,)),
                pltpu.SemaphoreType.DMA((MICRO,)),
                pltpu.SemaphoreType.DMA((MICRO,)),
                pltpu.SemaphoreType.DMA((MICRO, columns)),
                pltpu.SemaphoreType.DMA((MICRO, columns)),
                pltpu.SemaphoreType.DMA,
                pltpu.SemaphoreType.DMA,
                pltpu.SemaphoreType.DMA,
                pltpu.SemaphoreType.DMA,
            ],
            compiler_params=pltpu.CompilerParams(
                collective_id=0, has_side_effects=True, vmem_limit_bytes=48 << 20
            ),
            name="routed_backward",
        )(routes[0].T, router_probs[0].T, w_router.T, grad_sent, saved_hidden, w_down)

    placed = (
        P("pipe", "expert", None),
        P("pipe", "expert", None),
        P("pipe", "expert", None),
        P("pipe", "expert", None),
        P("expert", None, None),
        P(),
    )
    return jax.shard_map(
        on_device,
        mesh=mesh,
        in_specs=placed,
        out_specs=(P("pipe", "expert", None), P("pipe", "expert", None)),
        check_vma=False,
    )
```

time: 214 us -> 118 us (0.55)
  Pallas kernels: 0 us -> 109 us
  waiting for transfers between devices: 82.1 us -> 0 us
  local copies, waits for them, and re-layouts: 65.5 us -> 7.98 us
  starting transfers between devices: 51 us -> 0 us
  other arithmetic: 8.36 us -> 0 us
  matrix products: 3.77 us -> 0 us
    pallas_call x0 -> x1, Pallas kernels: none -> 109 us  [on_device(): pl.pallas_call(functools.partial(kernel, columns, depth), out_shape=(jax....]
    all_to_all x3 -> x0, waiting for transfers between devices: 82.1 us -> none  [the longest x1 69.4 us: on_device(): lax.all_to_all(send_rows, 'expert', split_axis=1, concat_axis=1, tiled=True)]
    scatter x4 -> x0, local copies, waits for them, and re-layouts: 37.7 us -> none  [the longest x2 12.7 us: on_device(): jnp.zeros((MICRO, send_width), jnp.bool_).at[micro_index, position]]
    all_to_all x3 -> x0, starting transfers between devices: 36.8 us -> none  [the longest x1 14.9 us: on_device(): lax.all_to_all(send_rows, 'expert', split_axis=1, concat_axis=1, tiled=True)]
    gather x10 -> x0, local copies, waits for them, and re-layouts: 20.9 us -> none  [the longest x2 15.8 us: on_device(): picked = jnp.take_along_axis(micro_grad, slot_token[..., None], axis=1)]
    ppermute x1 -> x0, starting transfers between devices: 14.2 us -> none  [from_behind(): return lax.ppermute(block, axis, route)]
    unnamed x13 -> x14, local copies, waits for them, and re-layouts: 0.94 us -> 7.98 us
    select_n x2 -> x0, other arithmetic: 5.12 us -> none  [the longest x1 5.12 us: on_device(): jnp.where(slot_used[..., None], picked, jnp.zeros((), jnp.bfloat16))]
  transfers between devices with their start and end apart: 4 -> 0, of which waited for: 2 -> 0; matrix products, arithmetic and copies ran while one was open for 31% -> 0% of each run, Pallas kernels for 0% -> 0%
where the time goes in v1:
time: 118 us; the launch traced here: 117 us
  Pallas kernels  109 us (92%)
  local copies, waits for them, and re-layouts  7.98 us (7%)
    pallas_call x1, Pallas kernels, on_device(): pl.pallas_call(functools.partial(kernel, columns, depth), out_shape=(jax....  109 us
    unnamed x14, local copies, waits for them, and re-layouts  7.98 us

profile of v1, /device:TPU:1, one launch (start us, length us, event | category | flops | bytes accessed | tf_op | source)
XLA Modules:
  0.0 117.3 jit_solution(9899558696159458147)
XLA Ops:
  0.6 0.0 copy-start
  0.6 1.9 %copy-done = bf16[1,768,2048]{2,1,0:T(8,128)(2,1)S(1)} copy-done((bf16[1,768,2048]{2,1,0:T(8,128)(2,1)S(1)}, bf16[1,768,2048]{2,1,0:T(8,128)(2,1)}, u32[]{:S(2)}) %copy-start) | copy-done | bytes 3145752
  2.5 0.0 copy-start.1
  2.5 1.1 copy-done.1
  3.6 0.0 copy-start.2
  3.6 1.0 copy-done.2
  4.6 0.0 copy-start.3
  4.6 0.9 copy-done.3
  5.6 0.0 copy-start.4
  5.6 0.8 copy-done.4
  6.3 0.0 copy-start.5
  6.3 0.7 copy-done.5
  7.0 108.6 %routed_backward.1 = (bf16[1,384,768]{2,1,0:T(8,128)(2,1)S(1)}, bf16[1,128,2048]{2,1,0:T(8,128)(2,1)S(1)}) custom-call(s32[2,128]{1,0:T(2,128)S(1)} %bitcast.9, f32[64,128]{1,0:T(8,128)S(1)} %bitcast.8, bf16[64,2048]{1,0:T(8,128)(2,1)S(1)} %bitcast.7, bf16[1,128,2048]{2,1,0:T(8,128)(2,1)S(1)} %copy-done.2, bf16[1,384,768]{2,1,0:T(8,128)(2,1)S(1)} %copy-done.1, ...), custom_call_target="tpu_custom_call" | custom-call | tf_op jit(solution)/shard_map/routed_backward/pallas_call | solution.py:311
  115.7 0.8 copy.10
  116.5 0.8 copy.11
Async XLA Ops:
  0.6 1.9 %copy-start = (bf16[1,768,2048]{2,1,0:T(8,128)(2,1)S(1)}, bf16[1,768,2048]{2,1,0:T(8,128)(2,1)}, u32[]{:S(2)}) copy-start(bf16[1,768,2048]{2,1,0:T(8,128)(2,1)} %weight_hbm.1) | copy-start | bytes 9437188
  2.5 1.1 copy-start.1
  3.6 1.0 copy-start.2
  4.6 0.9 copy-start.3
  5.6 0.8 copy-start.4
  6.3 0.7 copy-start.5

commit v2 on v0

v2 whole, which is shorter than its diff:
```python
import functools

import jax
import jax.numpy as jnp
from jax import lax
from jax.experimental import pallas as pl
from jax.experimental.pallas import tpu as pltpu
from jax.sharding import PartitionSpec as P

TOP = 2
MICRO = 2
CAP = 3
EACH = MICRO * CAP
NEAR = 3
LANES = 128
F32 = jnp.float32
BF16 = jnp.bfloat16


def iota(shape, axis):
    return lax.broadcasted_iota(jnp.int32, shape, axis)


def split(index, size):
    outer = lax.shift_right_logical(index * ((1 << 16) // size + 1), 16)
    return outer, index - outer * size


def onehot(condition):
    return condition.astype(F32).astype(BF16)


def dot(a, b, dims=((1,), (0,)), precision=None):
    return lax.dot_general(
        a, b, (dims, ((), ())), precision=precision, preferred_element_type=F32
    )


def kernel(
    columns,
    depth,
    routes_hbm,
    probs_hbm,
    router_hbm,
    grad_hbm,
    saved_hbm,
    weight_hbm,
    hidden_hbm,
    grad_in_hbm,
    routes_ref,
    probs_ref,
    router_ref,
    incoming,
    pick,
    order,
    place,
    apart,
    together,
    send,
    recv,
    saved,
    weight,
    scale_send,
    scale_recv,
    hidden,
    placed,
    grad_in,
    back_send,
    back_recv,
    load_sem,
    store_sem,
    pipe_send,
    pipe_recv,
    send_sem,
    recv_sem,
    scale_send_sem,
    scale_recv_sem,
    back_send_sem,
    back_recv_sem,
    column_ready,
    level_ready,
):
    experts = columns * depth
    half = depth // 2
    near = min(NEAR, half - 1)
    peers = 2 * columns
    rows = peers * EACH
    slots = half * rows
    tokens = incoming.shape[0] // MICRO
    all_tokens = MICRO * tokens
    groups = incoming.shape[1] // LANES
    unit = groups * EACH
    size = peers * unit
    pipes = lax.axis_size("pipe")
    stage = lax.axis_index("pipe")
    me = lax.axis_index("expert")
    column, level = me // depth, me % depth

    def expert_at(x, z):
        return (x % columns) * depth + z % depth

    beside = [{"expert": expert_at(column + step, level)} for step in (1, columns - 1)]
    along = [{"expert": expert_at(column, level + step)} for step in (1, depth - 1)]
    behind = {"pipe": (stage + pipes - 1) % pipes}
    ahead = {"pipe": (stage + 1) % pipes}

    barrier = pltpu.get_barrier_semaphore()
    for device in along + beside + [behind, ahead]:
        pl.semaphore_signal(barrier, inc=1, device_id=device)
    loads = [
        pltpu.make_async_copy(source, target, load_sem.at[at])
        for at, (source, target) in enumerate(
            (
                (routes_hbm, routes_ref),
                (probs_hbm, probs_ref),
                (saved_hbm.at[0], saved),
                (weight_hbm.at[0], weight),
                (router_hbm, router_ref),
            )
        )
    ]
    for load in loads:
        load.start()
    pl.semaphore_wait(barrier, 6)

    pipe_copy = pltpu.make_async_remote_copy(
        src_ref=grad_hbm.at[0],
        dst_ref=incoming,
        send_sem=pipe_send,
        recv_sem=pipe_recv,
        device_id=behind,
    )
    pipe_copy.start()
    for device in beside:
        pl.semaphore_signal(column_ready, inc=1, device_id=device)

    loads[0].wait()
    loads[1].wait()
    expert_row = iota((experts, all_tokens), 0)
    named = [(expert_row == routes_ref[k : k + 1, :]).astype(F32) for k in range(TOP)]
    probs = probs_ref[...]
    chosen = [jnp.sum(named[k] * probs, axis=0, keepdims=True) for k in range(TOP)]
    total = chosen[0] + chosen[1]
    weights = [chosen[k] / total for k in range(TOP)]
    before, after = iota((all_tokens, all_tokens), 0), iota((all_tokens, all_tokens), 1)
    earlier = (before < after) & ((before >= tokens) == (after >= tokens))
    seen = dot((named[0] + named[1]).astype(BF16), onehot(earlier))
    micro = (iota((1, all_tokens), 1) >= tokens).astype(F32)
    within = [
        micro * CAP + jnp.sum(named[k] * seen, axis=0, keepdims=True) for k in range(TOP)
    ]
    lane_row = iota((LANES, all_tokens), 0).astype(F32)
    slot = [(lane_row == within[k]).astype(F32) for k in range(TOP)]
    goal = [routes_ref[k : k + 1, :].astype(F32) * EACH + within[k] for k in range(TOP)]

    pl.semaphore_wait(column_ready, 2)

    def tell(step):
        for device in along:
            pl.semaphore_signal(level_ready.at[step], inc=1, device_id=device)

    tell(0)

    def levels(wave, sign):
        apart_by = jnp.where(wave == 0, half, wave)
        first = level + depth + sign * wave
        second = level + depth - sign * apart_by
        return first, second

    def peer_of(wave, peer, sign):
        first, second = levels(wave, sign)
        other = (peer >= columns).astype(jnp.int32)
        z = jnp.where(other == 1, second, first)
        z = z - jnp.where(z >= 2 * depth, 2 * depth, jnp.where(z >= depth, depth, 0))
        return (peer - other * columns) * depth + z

    def natural(index):
        wave, rest = split(index, rows)
        peer, each = split(rest, EACH)
        m, rank = split(each, CAP)
        return (m * experts + peer_of(wave, peer, -1)) * CAP + rank

    index = iota((slots, 1), 0)
    wave, rest = split(index, rows)
    peer, each = split(rest, EACH)
    wanted = (peer_of(wave, peer, 1) * EACH + each).astype(F32)
    pick[...] = onehot((wanted == goal[0]) | (wanted == goal[1]))
    order[...] = onehot(iota((slots, slots), 1) == natural(index))
    place[...] = onehot(iota((slots, slots), 0) == natural(iota((1, slots), 1)))
    line = iota((size, 1), 0)
    p, inner = split(line, unit)
    j, c = split(inner, EACH)
    apart[...] = onehot(iota((size, size), 1) == j * rows + p * EACH + c)
    j, inner = split(line, rows)
    p, c = split(inner, EACH)
    together[...] = onehot(iota((size, size), 1) == p * unit + j * EACH + c)
    scales = sum(
        dot(
            named[k].astype(BF16),
            (slot[k] * weights[k].astype(BF16).astype(F32)).astype(BF16),
            ((1,), (1,)),
        )
        for k in range(TOP)
    )
    wave, peer = split(iota((half * peers, 1), 0), peers)
    turned = onehot(iota((half * peers, experts), 1) == peer_of(wave, peer, 1))
    scale_send[...] = dot(turned, scales.astype(BF16)).reshape(half, peers, 1, LANES)

    def hear(step, carry):
        pl.semaphore_wait(level_ready.at[step], 2)
        tell(step + 1)
        return carry

    lax.fori_loop(0, near, hear, 0)
    pipe_copy.wait_recv()

    def wave_at(turn):
        return jnp.where(turn < near, turn + 1, jnp.where(turn == near, 0, half + near - turn))

    def visit(wave, sign, step):
        first, second = levels(wave, sign)
        other = step % 2
        x = (column + step // 2) % columns
        return other * columns + x, other * columns + column, expert_at(
            x, jnp.where(other == 1, second, first)
        )

    def row_copy(wave, step):
        there, here, device = visit(wave, 1, step)
        return pltpu.make_async_remote_copy(
            src_ref=send.at[wave, there],
            dst_ref=recv.at[wave, here],
            send_sem=send_sem.at[wave],
            recv_sem=recv_sem.at[wave],
            device_id={"expert": device},
        )

    def scale_copy(wave, step):
        there, here, device = visit(wave, 1, step)
        return pltpu.make_async_remote_copy(
            src_ref=scale_send.at[wave, there],
            dst_ref=scale_recv.at[wave, here],
            send_sem=scale_send_sem.at[wave],
            recv_sem=scale_recv_sem.at[wave],
            device_id={"expert": device},
        )

    def back_copy(wave, step):
        there, _, device = visit(wave, -1, step)
        return pltpu.make_async_remote_copy(
            src_ref=back_send.at[wave, there],
            dst_ref=back_recv.at[me],
            send_sem=back_send_sem,
            recv_sem=back_recv_sem,
            device_id={"expert": device},
        )

    def spread(turn, carry):
        wave = wave_at(turn)
        start = pl.multiple_of(wave * rows, 16)
        picked = dot(pick[pl.ds(start, rows), :], incoming[...]).astype(BF16)
        stacked = jnp.concatenate(
            [picked[:, j * LANES : (j + 1) * LANES] for j in range(groups)], axis=0
        )
        send[wave] = dot(apart[...], stacked).astype(BF16).reshape(peers, unit, LANES)
        others = jnp.where(wave == 0, 1, 0)

        def out(step, inner_carry):
            scale_copy(wave, step).start()
            row_copy(wave, step).start()
            return inner_carry

        lax.fori_loop(others, peers, out, 0)
        return carry

    lax.fori_loop(0, near, spread, 0)

    def hear_last(step, carry):
        hear(step, carry)
        return carry

    lax.fori_loop(near, half - 1, hear_last, 0)
    pl.semaphore_wait(level_ready.at[half - 1], 2)
    lax.fori_loop(near, half, spread, 0)
    pltpu.make_async_copy(scale_send.at[0, column], scale_recv.at[0, column], scale_recv_sem.at[0]).start()
    pltpu.make_async_copy(send.at[0, column], recv.at[0, column], recv_sem.at[0]).start()

    loads[2].wait()
    loads[3].wait()
    line_peer, line_slot = split(iota((rows, LANES), 0), EACH)
    ours = iota((rows, LANES), 1) == line_slot
    holder = onehot(split(iota((rows, peers), 0), EACH)[0] == iota((rows, peers), 1))
    holder_t = (split(iota((peers, rows), 1), EACH)[0] == iota((peers, rows), 0)).astype(F32)

    def gather(turn, carry):
        wave = wave_at(turn)
        start = pl.multiple_of(wave * rows, 16)
        held = dot(order[pl.ds(start, rows), :], saved[...])
        pltpu.make_async_copy(scale_send.at[wave], scale_recv.at[wave], scale_recv_sem.at[wave]).wait()
        all_scales = scale_recv[wave].reshape(peers, LANES).astype(BF16)
        scale = jnp.sum(jnp.where(ours, dot(holder, all_scales), 0.0), axis=1, keepdims=True)
        pltpu.make_async_copy(send.at[wave], recv.at[wave], recv_sem.at[wave]).wait()
        mixed = dot(together[...], recv[wave].reshape(size, LANES)).astype(BF16)
        flat = jnp.concatenate(
            [mixed[j * rows : (j + 1) * rows] for j in range(groups)], axis=1
        )
        grad = dot(flat, weight[...], ((1,), (1,)))
        route_grad = jnp.sum(grad * held, axis=1, keepdims=True)
        sums = dot(holder_t, jnp.where(ours, route_grad, 0.0), precision=lax.Precision.HIGHEST)
        back_send[wave] = sums.reshape(peers, 1, LANES)
        others = jnp.where(wave == 0, 1, 0)

        def back(step, inner_carry):
            back_copy(wave, step).start()
            return inner_carry

        lax.fori_loop(others, peers, back, 0)
        hidden[pl.ds(start, rows), :] = (scale * grad).astype(BF16)
        return carry

    lax.fori_loop(0, half, gather, 0)
    pltpu.make_async_copy(back_send.at[0, column], back_recv.at[me], back_recv_sem).start()
    placed[...] = dot(place[...], hidden[...]).astype(BF16)
    store_hidden = pltpu.make_async_copy(placed, hidden_hbm.at[0], store_sem.at[0])
    store_hidden.start()

    pipe_copy.wait_send()

    def left(wave, carry):
        pltpu.make_async_copy(send.at[wave], recv.at[wave], send_sem.at[wave]).wait()
        pltpu.make_async_copy(scale_send.at[wave], scale_recv.at[wave], scale_send_sem.at[wave]).wait()
        return carry

    lax.fori_loop(1, half, left, 0)
    remote = pl.ds(0, peers - 1)
    pltpu.make_async_copy(send.at[0, remote], recv.at[0, remote], send_sem.at[0]).wait()
    pltpu.make_async_copy(scale_send.at[0, remote], scale_recv.at[0, remote], scale_send_sem.at[0]).wait()
    loads[4].wait()

    pltpu.make_async_copy(back_recv, back_recv, back_recv_sem).wait()
    returned = back_recv[...].reshape(experts, LANES)
    slot_grad = [
        jnp.sum(
            slot[k] * dot(returned, named[k], ((0,), (0,)), lax.Precision.HIGHEST),
            axis=0,
            keepdims=True,
        )
        for k in range(TOP)
    ]
    mean = weights[0] * slot_grad[0] + weights[1] * slot_grad[1]
    logit = sum(named[k] * (weights[k] * (slot_grad[k] - mean)) for k in range(TOP))
    logit = logit.T
    high = logit.astype(BF16)
    low = (logit - high.astype(F32)).astype(BF16)
    router = router_ref[...]
    grad_in[...] = (dot(high, router) + dot(low, router)).astype(BF16)
    store_grad = pltpu.make_async_copy(grad_in, grad_in_hbm.at[0], store_sem.at[1])
    store_grad.start()
    others = pl.ds(0, experts - 1)
    pltpu.make_async_copy(back_recv.at[others], back_recv.at[others], back_send_sem).wait()
    store_hidden.wait()
    store_grad.wait()


def solution(mesh):
    experts = mesh.shape["expert"]
    depth = 16 if experts % 16 == 0 else 4

    def on_device(grad_sent, routes, router_probs, saved_hidden, w_down, w_router):
        all_tokens, model_width = grad_sent.shape[1:]
        slots, width = saved_hidden.shape[1:]
        columns = experts // depth
        half = depth // 2
        peers = 2 * columns
        unit = model_width // LANES * EACH
        in_place = pl.BlockSpec(memory_space=pl.ANY)
        dma = pltpu.SemaphoreType.DMA
        return pl.pallas_call(
            functools.partial(kernel, columns, depth),
            out_shape=(
                jax.ShapeDtypeStruct((1, slots, width), BF16),
                jax.ShapeDtypeStruct((1, all_tokens, model_width), BF16),
            ),
            in_specs=[in_place] * 6,
            out_specs=(in_place, in_place),
            scratch_shapes=[
                pltpu.VMEM((TOP, all_tokens), jnp.int32),
                pltpu.VMEM((experts, all_tokens), F32),
                pltpu.VMEM((experts, model_width), BF16),
                pltpu.VMEM((all_tokens, model_width), BF16),
                pltpu.VMEM((slots, all_tokens), BF16),
                pltpu.VMEM((slots, slots), BF16),
                pltpu.VMEM((slots, slots), BF16),
                pltpu.VMEM((peers * unit, peers * unit), BF16),
                pltpu.VMEM((peers * unit, peers * unit), BF16),
                pltpu.VMEM((half, peers, unit, LANES), BF16),
                pltpu.VMEM((half, peers, unit, LANES), BF16),
                pltpu.VMEM((slots, width), BF16),
                pltpu.VMEM((width, model_width), BF16),
                pltpu.VMEM((half, peers, 1, LANES), F32),
                pltpu.VMEM((half, peers, 1, LANES), F32),
                pltpu.VMEM((slots, width), BF16),
                pltpu.VMEM((slots, width), BF16),
                pltpu.VMEM((all_tokens, model_width), BF16),
                pltpu.VMEM((half, peers, 1, LANES), F32),
                pltpu.VMEM((experts, 1, LANES), F32),
                dma((5,)),
                dma((2,)),
                dma,
                dma,
                dma((half,)),
                dma((half,)),
                dma((half,)),
                dma((half,)),
                dma,
                dma,
                pltpu.SemaphoreType.REGULAR,
                pltpu.SemaphoreType.REGULAR((half,)),
            ],
            compiler_params=pltpu.CompilerParams(
                collective_id=0, has_side_effects=True, vmem_limit_bytes=67043328
            ),
            name="routed_backward",
        )(routes[0].T, router_probs[0].T, w_router.T, grad_sent, saved_hidden, w_down)

    placed = (
        P("pipe", "expert", None),
        P("pipe", "expert", None),
        P("pipe", "expert", None),
        P("pipe", "expert", None),
        P("expert", None, None),
        P(),
    )
    return jax.shard_map(
        on_device,
        mesh=mesh,
        in_specs=placed,
        out_specs=(P("pipe", "expert", None), P("pipe", "expert", None)),
        check_vma=False,
    )
```

time: 214 us -> 117 us (0.55); the launches traced: 212 us -> 117 us
  Pallas kernels: 0 us -> 113 us
  waiting for transfers between devices: 82.1 us -> 0 us
  local copies, waits for them, and re-layouts: 65.5 us -> 3.8 us
  starting transfers between devices: 51 us -> 0 us
  other arithmetic: 8.36 us -> 0 us
  matrix products: 3.77 us -> 0 us
    pallas_call x0 -> x1, Pallas kernels: none -> 113 us  [on_device(): pl.pallas_call(functools.partial(kernel, columns, depth), out_shape=(jax....]
    all_to_all x3 -> x0, waiting for transfers between devices: 82.1 us -> none  [the longest x1 69.4 us: on_device(): lax.all_to_all(send_rows, 'expert', split_axis=1, concat_axis=1, tiled=True)]
    scatter x4 -> x0, local copies, waits for them, and re-layouts: 37.7 us -> none  [the longest x2 12.7 us: on_device(): jnp.zeros((MICRO, send_width), jnp.bool_).at[micro_index, position]]
    all_to_all x3 -> x0, starting transfers between devices: 36.8 us -> none  [the longest x1 14.9 us: on_device(): lax.all_to_all(send_rows, 'expert', split_axis=1, concat_axis=1, tiled=True)]
    gather x10 -> x0, local copies, waits for them, and re-layouts: 20.9 us -> none  [the longest x2 15.8 us: on_device(): picked = jnp.take_along_axis(micro_grad, slot_token[..., None], axis=1)]
    ppermute x1 -> x0, starting transfers between devices: 14.2 us -> none  [from_behind(): return lax.ppermute(block, axis, route)]
    select_n x2 -> x0, other arithmetic: 5.12 us -> none  [the longest x1 5.12 us: on_device(): jnp.where(slot_used[..., None], picked, jnp.zeros((), jnp.bfloat16))]
    all_to_all x8 -> x0, local copies, waits for them, and re-layouts: 4.02 us -> none  [the longest x1 2.09 us: on_device(): lax.all_to_all(send_rows, 'expert', split_axis=1, concat_axis=1, tiled=True)]
  transfers between devices with their start and end apart: 4 -> 0, of which waited for: 2 -> 0; matrix products, arithmetic and copies ran while one was open for 31% -> 0% of each run, Pallas kernels for 0% -> 0%
where the time goes in v2:
time: 117 us
  Pallas kernels  113 us (97%)
  local copies, waits for them, and re-layouts  3.8 us (3%)
    pallas_call x1, Pallas kernels, on_device(): pl.pallas_call(functools.partial(kernel, columns, depth), out_shape=(jax....  113 us
    unnamed x2, local copies, waits for them, and re-layouts  3.8 us

profile of v2, /device:TPU:1, one launch (start us, length us, event | category | flops | bytes accessed | tf_op | source)
XLA Modules:
  0.0 117.1 jit_solution(13169491681370377528)
XLA Ops:
  0.6 112.7 %routed_backward.1 = (bf16[1,384,768]{2,1,0:T(8,128)(2,1)}, bf16[1,128,2048]{2,1,0:T(8,128)(2,1)}) custom-call(s32[2,128]{1,0:T(2,128)} %bitcast.9, f32[64,128]{1,0:T(8,128)} %bitcast.8, bf16[64,2048]{1,0:T(8,128)(2,1)} %bitcast.7, bf16[1,128,2048]{2,1,0:T(8,128)(2,1)} %grad_hbm.1, bf16[1,384,768]{2,1,0:T(8,128)(2,1)} %saved_hbm.1, ...), custom_call_target="tpu_custom_call" | custom-call | tf_op jit(solution)/shard_map/routed_backward/pallas_call | solution.py:378
  113.3 1.9 %copy.10 = bf16[1,384,768]{2,1,0:T(8,128)(2,1)} copy(bf16[1,384,768]{2,1,0:T(8,128)(2,1)} %get-tuple-element.4) | data formatting | bytes 1179648
  115.2 1.9 %copy.11 = bf16[1,128,2048]{2,1,0:T(8,128)(2,1)} copy(bf16[1,128,2048]{2,1,0:T(8,128)(2,1)} %get-tuple-element.5) | data formatting | bytes 1048576

commit v3 on v1

--- a/solution.py
+++ b/solution.py
@@ -19,6 +19,15 @@
     return lax.broadcasted_iota(jnp.int32, shape, axis)
 
 
+def split(index, size):
+    outer = lax.shift_right_logical(index * ((1 << 16) // size + 1), 16)
+    return outer, index - outer * size
+
+
+def onehot(condition):
+    return condition.astype(F32).astype(BF16)
+
+
 def dot(a, b, dims=((1,), (0,)), precision=None):
     return lax.dot_general(
         a, b, (dims, ((), ())), precision=precision, preferred_element_type=F32
@@ -28,14 +37,15 @@
 def kernel(
     columns,
     depth,
+    routes_hbm,
+    probs_hbm,
+    grad_hbm,
+    saved_hbm,
+    weight_hbm,
+    hidden_hbm,
+    logit_ref,
     routes_ref,
     probs_ref,
-    router_ref,
-    grad_ref,
-    saved_hbm,
-    weight_hbm,
-    hidden_ref,
-    grad_in_ref,
     incoming,
     pick,
     swap,
@@ -46,9 +56,11 @@
     scale_send,
     scale_recv,
     partial,
+    hidden,
     back_send,
     back_recv,
     load_sem,
+    store_sem,
     pipe_send,
     pipe_recv,
     send_sem,
@@ -57,32 +69,64 @@
     scale_recv_sem,
     back_send_sem,
     back_recv_sem,
+    column_ready,
+    level_ready,
 ):
     experts = columns * depth
     slab = depth * CAP
     tokens = incoming.shape[1]
     groups = incoming.shape[2] // LANES
     unit = groups * CAP
+    size = slab * groups
     pipes = lax.axis_size("pipe")
     stage = lax.axis_index("pipe")
     me = lax.axis_index("expert")
     column, level = me // depth, me % depth
 
+    def expert_at(x, z):
+        return {"expert": (x % columns) * depth + z % depth}
+
+    def along(distance):
+        return [expert_at(column, level + step) for step in (distance, depth - distance)]
+
+    beside = [expert_at(column + step, level) for step in (1, columns - 1)]
+    behind = {"pipe": (stage + pipes - 1) % pipes}
+    ahead = {"pipe": (stage + 1) % pipes}
+
     barrier = pltpu.get_barrier_semaphore()
-
-    def greet(step, carry):
-        pl.semaphore_signal(barrier, inc=1, device_id={"expert": (me + step) % experts})
-        return carry
-
-    lax.fori_loop(1, experts, greet, 0)
-    for distance in (1, pipes - 1):
-        pl.semaphore_signal(barrier, inc=1, device_id={"pipe": (stage + distance) % pipes})
-
-    load_weight = pltpu.make_async_copy(weight_hbm.at[0], weight, load_sem.at[0])
-    load_saved = pltpu.make_async_copy(saved_hbm.at[0], saved, load_sem.at[1])
-    load_weight.start()
-    load_saved.start()
-
+    for device in along(1) + beside + [behind, ahead]:
+        pl.semaphore_signal(barrier, inc=1, device_id=device)
+    loads = [
+        pltpu.make_async_copy(source, target, load_sem.at[at])
+        for at, (source, target) in enumerate(
+            (
+                (routes_hbm, routes_ref),
+                (probs_hbm, probs_ref),
+                (saved_hbm.at[0], saved),
+                (weight_hbm.at[0], weight),
+            )
+        )
+    ]
+    for load in loads:
+        load.start()
+    pl.semaphore_wait(barrier, 6)
+
+    def pipe_copy(m):
+        return pltpu.make_async_remote_copy(
+            src_ref=grad_hbm.at[0, pl.ds(m * tokens, tokens)],
+            dst_ref=incoming.at[m],
+            send_sem=pipe_send.at[m],
+            recv_sem=pipe_recv.at[m],
+            device_id=behind,
+        )
+
+    for m in range(MICRO):
+        pipe_copy(m).start()
+    for device in beside:
+        pl.semaphore_signal(column_ready, inc=1, device_id=device)
+
+    loads[0].wait()
+    loads[1].wait()
     all_tokens = MICRO * tokens
     expert_row = iota((experts, all_tokens), 0)
     named = [(expert_row == routes_ref[k : k + 1, :]).astype(F32) for k in range(TOP)]
@@ -92,11 +136,36 @@
     weights = [chosen[k] / total for k in range(TOP)]
     before, after = iota((all_tokens, all_tokens), 0), iota((all_tokens, all_tokens), 1)
     earlier = (before < after) & ((before >= tokens) == (after >= tokens))
-    seen = dot((named[0] + named[1]).astype(BF16), earlier.astype(F32).astype(BF16))
+    seen = dot((named[0] + named[1]).astype(BF16), onehot(earlier))
     rank = [jnp.sum(named[k] * seen, axis=0, keepdims=True) for k in range(TOP)]
+    row = [routes_ref[k : k + 1, :].astype(F32) * CAP + rank[k] for k in range(TOP)]
+
+    rounds = [1] + [1 << at for at in range(depth.bit_length() - 2)]
+
+    def tell(at):
+        for device in along(rounds[at]):
+            pl.semaphore_signal(level_ready.at[at], inc=1, device_id=device)
+
+    def hear(at):
+        pl.semaphore_wait(level_ready.at[at], 2)
+
+    pl.semaphore_wait(column_ready, 2)
+    tell(0)
+    for m in range(MICRO):
+        here = iota((experts * CAP, tokens), 0).astype(F32)
+        part = [row[k][:, m * tokens : (m + 1) * tokens] for k in range(TOP)]
+        pick[m] = onehot((here == part[0]) | (here == part[1]))
+    hear(0)
+    tell(1)
     micro = (iota((1, all_tokens), 1) >= tokens).astype(F32)
     lane_row = iota((LANES, all_tokens), 0).astype(F32)
     slot = [(lane_row == micro * CAP + rank[k]).astype(F32) for k in range(TOP)]
+    outer, inner = split(iota((size, 1), 0), unit)
+    third, own = split(inner, CAP)
+    swap[...] = onehot(iota((size, size), 1) == third * unit + outer * CAP + own)
+    for at in range(1, len(rounds) - 1):
+        hear(at)
+        tell(at + 1)
     scales = sum(
         dot(
             named[k].astype(BF16),
@@ -106,33 +175,6 @@
         for k in range(TOP)
     )
     scale_send[...] = scales.reshape(experts, 1, LANES)
-    row = [routes_ref[k : k + 1, :].astype(F32) * CAP + rank[k] for k in range(TOP)]
-    for m in range(MICRO):
-        here = iota((experts * CAP, tokens), 0).astype(F32)
-        part = [row[k][:, m * tokens : (m + 1) * tokens] for k in range(TOP)]
-        pick[m] = ((here == part[0]) | (here == part[1])).astype(F32).astype(BF16)
-
-    size = slab * groups
-    index = iota((size, 1), 0)
-    outer = lax.shift_right_logical(index * ((1 << 16) // unit + 1), 16)
-    inner = index - outer * unit
-    third = lax.shift_right_logical(inner * ((1 << 16) // CAP + 1), 16)
-    target = third * unit + outer * CAP + (inner - third * CAP)
-    swap[...] = (iota((size, size), 1) == target).astype(F32).astype(BF16)
-
-    pl.semaphore_wait(barrier, experts - 1 + 2)
-
-    def pipe_copy(m):
-        return pltpu.make_async_remote_copy(
-            src_ref=grad_ref.at[0, pl.ds(m * tokens, tokens)],
-            dst_ref=incoming.at[m],
-            send_sem=pipe_send.at[m],
-            recv_sem=pipe_recv.at[m],
-            device_id={"pipe": (stage + pipes - 1) % pipes},
-        )
-
-    for m in range(MICRO):
-        pipe_copy(m).start()
 
     def scale_copy(peer):
         return pltpu.make_async_remote_copy(
@@ -147,9 +189,6 @@
         scale_copy((me + step) % experts).start()
         return carry
 
-    lax.fori_loop(1, experts, scale_out, 0)
-    pltpu.make_async_copy(scale_send.at[me], scale_recv.at[me], scale_recv_sem).start()
-
     def row_copy(m, far, to):
         return pltpu.make_async_remote_copy(
             src_ref=send.at[m, far, to],
@@ -174,27 +213,43 @@
         mixed = dot(swap[...], stacked).astype(BF16)
         send[m, far] = mixed.reshape(depth, unit, LANES)
 
-    for m in range(MICRO):
-        pipe_copy(m).wait_recv()
-
-        def spread(turn, carry):
+    def spread(m, first_step, last_step, packs):
+        def body(turn, carry):
             far = (column + turn) % columns
-            fill(m, far)
+            if packs:
+                fill(m, far)
 
             def out(step, inner_carry):
                 row_copy(m, far, hop(step)).start()
                 return inner_carry
 
-            lax.fori_loop(0, jnp.where(turn == 0, depth - 1, depth), out, 0)
+            end = last_step
+            if last_step == depth:
+                end = jnp.where(turn == 0, depth - 1, depth)
+            lax.fori_loop(first_step, end, out, 0)
             return carry
 
-        lax.fori_loop(0, columns, spread, 0)
+        lax.fori_loop(0, columns, body, 0)
+
+    def stay(m):
         pltpu.make_async_copy(
             send.at[m, column, level], recv.at[m, column, level], recv_sem.at[m, column]
         ).start()
 
-    load_weight.wait()
-    load_saved.wait()
+    far_steps = depth // 2 - 1
+    pipe_copy(0).wait_recv()
+    spread(0, far_steps, depth, True)
+    hear(len(rounds) - 1)
+    spread(0, 0, far_steps, False)
+    lax.fori_loop(1, experts, scale_out, 0)
+    pltpu.make_async_copy(scale_send.at[me], scale_recv.at[me], scale_recv_sem).start()
+    pipe_copy(1).wait_recv()
+    spread(1, 0, depth, True)
+    for m in range(MICRO):
+        stay(m)
+
+    loads[2].wait()
+    loads[3].wait()
     pltpu.make_async_copy(scale_send, scale_recv, scale_recv_sem).wait()
 
     owner = iota((slab, depth), 0)
@@ -238,7 +293,9 @@
             all_scales = scale_recv[pl.ds(first, depth)].reshape(depth, LANES)
             spread_scales = dot(holder.astype(BF16), all_scales.astype(BF16))
             scale = jnp.sum(jnp.where(ours, spread_scales, 0.0), axis=1, keepdims=True)
-            hidden_ref[0, pl.ds(start, slab), :] = (scale * grad).astype(BF16)
+            hidden[pl.ds(start, slab), :] = (scale * grad).astype(BF16)
+            stored = pl.ds(start, slab)
+            pltpu.make_async_copy(hidden.at[stored], hidden_hbm.at[stored], store_sem).start()
             sums = dot(
                 holder_t, jnp.where(ours, route_grad, 0.0), precision=lax.Precision.HIGHEST
             )
@@ -287,12 +344,35 @@
     ]
     mean = weights[0] * slot_grad[0] + weights[1] * slot_grad[1]
     logit = sum(named[k] * (weights[k] * (slot_grad[k] - mean)) for k in range(TOP))
-    logit = logit.T
-    high = logit.astype(BF16)
-    low = (logit - high.astype(F32)).astype(BF16)
-    router = router_ref[...]
-    grad_in_ref[0] = (dot(high, router) + dot(low, router)).astype(BF16)
+    logit_ref[...] = logit
     pltpu.make_async_copy(back_send.at[others], back_recv.at[others], back_send_sem).wait()
+    pltpu.make_async_copy(hidden, hidden_hbm, store_sem).wait()
+
+
+def finish(hidden_hbm, logit_hbm, router_hbm, out_hbm, grad_in_hbm, hidden, logit, router, grad_in, sem):
+    loads = [
+        pltpu.make_async_copy(source, target, sem.at[at])
+        for at, (source, target) in enumerate(
+            ((hidden_hbm, hidden), (logit_hbm, logit), (router_hbm, router))
+        )
+    ]
+    for load in loads:
+        load.start()
+    loads[0].wait()
+    stores = [
+        pltpu.make_async_copy(hidden, out_hbm.at[0], sem.at[3]),
+        pltpu.make_async_copy(grad_in, grad_in_hbm.at[0], sem.at[4]),
+    ]
+    stores[0].start()
+    loads[1].wait()
+    by_token = logit[...].T
+    high = by_token.astype(BF16)
+    low = (by_token - high.astype(F32)).astype(BF16)
+    loads[2].wait()
+    grad_in[...] = (dot(high, router[...]) + dot(low, router[...])).astype(BF16)
+    stores[1].start()
+    for store in stores:
+        store.wait()
 
 
 def solution(mesh):
@@ -308,15 +388,17 @@
         unit = depth * CAP
         in_vmem = pl.BlockSpec(memory_space=pltpu.VMEM)
         in_place = pl.BlockSpec(memory_space=pl.ANY)
-        return pl.pallas_call(
+        hidden, logit = pl.pallas_call(
             functools.partial(kernel, columns, depth),
             out_shape=(
-                jax.ShapeDtypeStruct((1, slots, width), BF16),
-                jax.ShapeDtypeStruct((1, MICRO * tokens, model_width), BF16),
+                jax.ShapeDtypeStruct((slots, width), BF16),
+                jax.ShapeDtypeStruct((experts, MICRO * tokens), F32),
             ),
-            in_specs=[in_vmem, in_vmem, in_vmem, in_place, in_place, in_place],
-            out_specs=(in_vmem, in_vmem),
+            in_specs=[in_place] * 5,
+            out_specs=(in_place, in_vmem),
             scratch_shapes=[
+                pltpu.VMEM((TOP, MICRO * tokens), jnp.int32),
+                pltpu.VMEM((experts, MICRO * tokens), F32),
                 pltpu.VMEM((MICRO, tokens, model_width), BF16),
                 pltpu.VMEM((MICRO, experts * CAP, tokens), BF16),
                 pltpu.VMEM((slab * depth, slab * depth), BF16),
@@ -327,9 +409,11 @@
                 pltpu.VMEM((experts, 1, LANES), F32),
                 pltpu.VMEM((experts, 1, LANES), F32),
                 pltpu.VMEM((experts, LANES), F32),
+                pltpu.VMEM((slots, width), BF16),
                 pltpu.VMEM((experts, 1, LANES), F32),
                 pltpu.VMEM((experts, 1, LANES), F32),
-                pltpu.SemaphoreType.DMA((2,)),
+                pltpu.SemaphoreType.DMA((4,)),
+                pltpu.SemaphoreType.DMA,
                 pltpu.SemaphoreType.DMA((MICRO,)),
                 pltpu.SemaphoreType.DMA((MICRO,)),
                 pltpu.SemaphoreType.DMA((MICRO, columns)),
@@ -338,12 +422,32 @@
                 pltpu.SemaphoreType.DMA,
                 pltpu.SemaphoreType.DMA,
                 pltpu.SemaphoreType.DMA,
+                pltpu.SemaphoreType.REGULAR,
+                pltpu.SemaphoreType.REGULAR((depth.bit_length() - 1,)),
             ],
             compiler_params=pltpu.CompilerParams(
-                collective_id=0, has_side_effects=True, vmem_limit_bytes=48 << 20
+                collective_id=0, has_side_effects=True, vmem_limit_bytes=67043328
             ),
             name="routed_backward",
-        )(routes[0].T, router_probs[0].T, w_router.T, grad_sent, saved_hidden, w_down)
+        )(routes[0].T, router_probs[0].T, grad_sent, saved_hidden, w_down)
+        return pl.pallas_call(
+            finish,
+            out_shape=(
+                jax.ShapeDtypeStruct((1, slots, width), BF16),
+                jax.ShapeDtypeStruct((1, MICRO * tokens, model_width), BF16),
+            ),
+            in_specs=[in_place] * 3,
+            out_specs=(in_place, in_place),
+            scratch_shapes=[
+                pltpu.VMEM((slots, width), BF16),
+                pltpu.VMEM((experts, MICRO * tokens), F32),
+                pltpu.VMEM((experts, model_width), BF16),
+                pltpu.VMEM((MICRO * tokens, model_width), BF16),
+                pltpu.SemaphoreType.DMA((5,)),
+            ],
+            compiler_params=pltpu.CompilerParams(vmem_limit_bytes=67043328),
+            name="finish",
+        )(hidden, logit, w_router.T)
 
     placed = (
         P("pipe", "expert", None),

time: 118 us -> 112 us (0.949)
  the two profiles are of different devices: /device:TPU:1 before, /device:TPU:24 now
where the time goes in v3:
time: 112 us
  Pallas kernels  112 us (100%)
    pallas_call x1, Pallas kernels, on_device(): pl.pallas_call(functools.partial(kernel, columns, depth), out_shape=(jax....  109 us
    pallas_call x1, Pallas kernels, on_device(): pl.pallas_call(finish, out_shape=(jax.ShapeDtypeStruct((1, slots, width),...  2.42 us

profile of v3, /device:TPU:24, one launch (start us, length us, event | category | flops | bytes accessed | tf_op | source)
XLA Modules:
  0.0 112.2 jit_solution(143088388611308879)
XLA Ops:
  0.6 109.2 %routed_backward.1 = (bf16[384,768]{1,0:T(8,128)(2,1)}, f32[64,128]{1,0:T(8,128)}) custom-call(s32[2,128]{1,0:T(2,128)} %bitcast.9, f32[64,128]{1,0:T(8,128)} %bitcast.8, bf16[1,128,2048]{2,1,0:T(8,128)(2,1)} %grad_hbm.1, bf16[1,384,768]{2,1,0:T(8,128)(2,1)} %saved_hbm.1, bf16[1,768,2048]{2,1,0:T(8,128)(2,1)} %weight_hbm.1), custom_call_target="tpu_custom_call" | custom-call | tf_op jit(solution)/shard_map/routed_backward/pallas_call | solution.py:391
  109.8 2.4 %finish.1 = (bf16[1,384,768]{2,1,0:T(8,128)(2,1)}, bf16[1,128,2048]{2,1,0:T(8,128)(2,1)}) custom-call(bf16[384,768]{1,0:T(8,128)(2,1)} %get-tuple-element.4.hidden_hbm, f32[64,128]{1,0:T(8,128)} %get-tuple-element.5.logit_hbm, bf16[64,2048]{1,0:T(8,128)(2,1)} %bitcast.7), custom_call_target="tpu_custom_call" | custom-call | tf_op jit(solution)/shard_map/finish/pallas_call | solution.py:433

commit v4 on v3

v4 whole, which is shorter than its diff:
```python
import functools

import jax
import jax.numpy as jnp
from jax import lax
from jax.experimental import pallas as pl
from jax.experimental.pallas import tpu as pltpu
from jax.sharding import PartitionSpec as P

TOP = 2
MICRO = 2
CAP = 3
LANES = 128
F32 = jnp.float32
BF16 = jnp.bfloat16


def iota(shape, axis):
    return lax.broadcasted_iota(jnp.int32, shape, axis)


def split(index, size):
    outer = lax.shift_right_logical(index * ((1 << 16) // size + 1), 16)
    return outer, index - outer * size


def onehot(condition):
    return condition.astype(F32).astype(BF16)


def dot(a, b, dims=((1,), (0,)), precision=None):
    return lax.dot_general(
        a, b, (dims, ((), ())), precision=precision, preferred_element_type=F32
    )


def kernel(
    columns,
    depth,
    routes_hbm,
    probs_hbm,
    grad_hbm,
    saved_hbm,
    weight_hbm,
    hidden_hbm,
    logit_ref,
    routes_ref,
    probs_ref,
    incoming,
    pick,
    order,
    place,
    apart,
    together,
    send,
    recv,
    saved,
    aligned,
    weight,
    scale_send,
    scale_recv,
    hidden,
    placed,
    back_send,
    back_recv,
    load_sem,
    store_sem,
    pipe_send,
    pipe_recv,
    send_sem,
    recv_sem,
    scale_send_sem,
    scale_recv_sem,
    back_send_sem,
    back_recv_sem,
    column_ready,
    level_ready,
):
    experts = columns * depth
    half = depth // 2
    peers = 2 * columns
    rows = MICRO * peers * CAP
    slots = half * rows
    tokens = incoming.shape[1]
    groups = incoming.shape[2] // LANES
    unit = groups * CAP
    size = peers * unit
    first = [2, 3] if half > 3 else [1]
    last = [0] + [w for w in range(half - 1, 0, -1) if w not in first + [1]]
    last += [1] if 1 not in first else []
    waves = first + last
    pipes = lax.axis_size("pipe")
    stage = lax.axis_index("pipe")
    me = lax.axis_index("expert")
    column, level = me // depth, me % depth

    def expert_at(x, z):
        return {"expert": (x % columns) * depth + z % depth}

    def along(distance):
        return [expert_at(column, level + step) for step in (distance, depth - distance)]

    beside = [expert_at(column + step, level) for step in (1, columns - 1)]
    behind = {"pipe": (stage + pipes - 1) % pipes}
    ahead = {"pipe": (stage + 1) % pipes}

    barrier = pltpu.get_barrier_semaphore()
    for device in along(1) + beside + [behind, ahead]:
        pl.semaphore_signal(barrier, inc=1, device_id=device)
    loads = [
        pltpu.make_async_copy(source, target, load_sem.at[at])
        for at, (source, target) in enumerate(
            (
                (routes_hbm, routes_ref),
                (probs_hbm, probs_ref),
                (saved_hbm.at[0], saved),
                (weight_hbm.at[0], weight),
            )
        )
    ]
    for load in loads:
        load.start()
    pl.semaphore_wait(barrier, 6)

    def pipe_copy(m):
        return pltpu.make_async_remote_copy(
            src_ref=grad_hbm.at[0, pl.ds(m * tokens, tokens)],
            dst_ref=incoming.at[m],
            send_sem=pipe_send.at[m],
            recv_sem=pipe_recv.at[m],
            device_id=behind,
        )

    for m in range(MICRO):
        pipe_copy(m).start()
    for device in beside:
        pl.semaphore_signal(column_ready, inc=1, device_id=device)

    loads[0].wait()
    loads[1].wait()
    all_tokens = MICRO * tokens
    expert_row = iota((experts, all_tokens), 0)
    named = [(expert_row == routes_ref[k : k + 1, :]).astype(F32) for k in range(TOP)]
    probs = probs_ref[...]
    chosen = [jnp.sum(named[k] * probs, axis=0, keepdims=True) for k in range(TOP)]
    total = chosen[0] + chosen[1]
    weights = [chosen[k] / total for k in range(TOP)]
    before, after = iota((all_tokens, all_tokens), 0), iota((all_tokens, all_tokens), 1)
    earlier = (before < after) & ((before >= tokens) == (after >= tokens))
    seen = dot((named[0] + named[1]).astype(BF16), onehot(earlier))
    rank = [jnp.sum(named[k] * seen, axis=0, keepdims=True) for k in range(TOP)]
    row = [routes_ref[k : k + 1, :].astype(F32) * CAP + rank[k] for k in range(TOP)]

    rounds = [1] + [1 << at for at in range(depth.bit_length() - 2)]

    def tell(at):
        for device in along(rounds[at]):
            pl.semaphore_signal(level_ready.at[at], inc=1, device_id=device)

    def hear(at):
        pl.semaphore_wait(level_ready.at[at], 2)

    pl.semaphore_wait(column_ready, 2)
    tell(0)

    def levels(wave, sign):
        other = jnp.where(wave == 0, half, wave)
        return level + depth + sign * wave, level + depth - sign * other

    def peer_of(wave, peer, sign):
        direct, opposite = levels(wave, sign)
        other = (peer >= columns).astype(jnp.int32)
        z = jnp.where(other == 1, opposite, direct)
        z = z - jnp.where(z >= 2 * depth, 2 * depth, jnp.where(z >= depth, depth, 0))
        return (peer - other * columns) * depth + z

    wave, rest = split(iota((slots // MICRO, 1), 0), peers * CAP)
    peer, own = split(rest, CAP)
    wanted = (peer_of(wave, peer, 1) * CAP + own).astype(F32)
    for m in range(MICRO):
        part = [row[k][:, m * tokens : (m + 1) * tokens] for k in range(TOP)]
        pick[m] = onehot((wanted == part[0]) | (wanted == part[1])).reshape(half, peers * CAP, tokens)
    hear(0)
    tell(1)
    micro = (iota((1, all_tokens), 1) >= tokens).astype(F32)
    lane_row = iota((LANES, all_tokens), 0).astype(F32)
    slot = [(lane_row == micro * CAP + rank[k]).astype(F32) for k in range(TOP)]
    p, inner = split(iota((size, 1), 0), unit)
    j, own = split(inner, CAP)
    apart[...] = onehot(iota((size, size), 1) == j * (peers * CAP) + p * CAP + own)
    for at in range(1, len(rounds) - 1):
        hear(at)
        tell(at + 1)
    scales = sum(
        dot(
            named[k].astype(BF16),
            (slot[k] * weights[k].astype(BF16).astype(F32)).astype(BF16),
            ((1,), (1,)),
        )
        for k in range(TOP)
    )
    wave, peer = split(iota((half * peers, 1), 0), peers)
    turned = onehot(iota((half * peers, experts), 1) == peer_of(wave, peer, 1))
    scale_send[...] = dot(turned, scales.astype(BF16)).reshape(half, peers, 1, LANES)

    def wave_at(turn):
        wave = waves[0]
        for at in range(1, half):
            wave = jnp.where(turn == at, waves[at], wave)
        return wave

    def visit(wave, sign, step):
        direct, opposite = levels(wave, sign)
        other = step % 2
        x = (column + step // 2) % columns
        z = jnp.where(other == 1, opposite, direct)
        return other * columns + x, other * columns + column, expert_at(x, z)

    def row_copy(wave, m, step):
        there, here, device = visit(wave, 1, step)
        return pltpu.make_async_remote_copy(
            src_ref=send.at[wave, m, there],
            dst_ref=recv.at[wave, m, here],
            send_sem=send_sem.at[wave],
            recv_sem=recv_sem.at[wave],
            device_id=device,
        )

    def scale_copy(wave, step):
        there, here, device = visit(wave, 1, step)
        return pltpu.make_async_remote_copy(
            src_ref=scale_send.at[wave, there],
            dst_ref=scale_recv.at[wave, here],
            send_sem=scale_send_sem.at[wave],
            recv_sem=scale_recv_sem.at[wave],
            device_id=device,
        )

    def back_copy(wave, step):
        there, _, device = visit(wave, -1, step)
        return pltpu.make_async_remote_copy(
            src_ref=back_send.at[wave, there],
            dst_ref=back_recv.at[me],
            send_sem=back_send_sem,
            recv_sem=back_recv_sem,
            device_id=device,
        )

    def others(wave):
        return jnp.where(wave == 0, 1, 0)

    def spread(m, turn):
        wave = wave_at(turn)
        picked = dot(pick[m, wave], incoming[m])
        stacked = jnp.concatenate(
            [picked[:, j * LANES : (j + 1) * LANES] for j in range(groups)], axis=0
        ).astype(BF16)
        send[wave, m] = dot(apart[...], stacked).astype(BF16).reshape(peers, unit, LANES)

        def out(step, carry):
            row_copy(wave, m, step).start()
            return carry

        lax.fori_loop(others(wave), peers, out, 0)

    def spread_first(m):
        def body(turn, carry):
            spread(m, turn)
            return carry

        lax.fori_loop(0, len(first), body, 0)

    def spread_last(index, carry):
        turn, m = index // MICRO, index % MICRO
        spread(m, turn)
        return carry

    def spread_scales(index, carry):
        wave, step = index // peers, index % peers
        scale_copy(wave, step).start()
        return carry

    for m in range(MICRO):
        pipe_copy(m).wait_recv()
        spread_first(m)
    hear(len(rounds) - 1)
    lax.fori_loop(1, half * peers, spread_scales, 0)
    lax.fori_loop(len(first) * MICRO, half * MICRO, spread_last, 0)
    pltpu.make_async_copy(scale_send.at[0, column], scale_recv.at[0, column], scale_recv_sem.at[0]).start()
    for m in range(MICRO):
        pltpu.make_async_copy(
            send.at[0, m, column], recv.at[0, m, column], recv_sem.at[0]
        ).start()

    def natural(index):
        wave, rest = split(index, rows)
        m, rest = split(rest, peers * CAP)
        peer, own = split(rest, CAP)
        return (m * experts + peer_of(wave, peer, -1)) * CAP + own

    order[...] = onehot(iota((slots, slots), 1) == natural(iota((slots, 1), 0)))
    place[...] = onehot(iota((slots, slots), 0) == natural(iota((1, slots), 1)))
    j, inner = split(iota((MICRO * size, 1), 0), rows)
    m, inner = split(inner, peers * CAP)
    p, own = split(inner, CAP)
    together[...] = onehot(
        iota((MICRO * size, MICRO * size), 1) == m * size + p * unit + j * CAP + own
    )

    def peer_and_slot(line):
        m, inner = split(line, peers * CAP)
        p, own = split(inner, CAP)
        return p, m * CAP + own

    ours = iota((rows, LANES), 1) == peer_and_slot(iota((rows, LANES), 0))[1]
    holder = onehot(peer_and_slot(iota((rows, peers), 0))[0] == iota((rows, peers), 1))
    holder_t = (peer_and_slot(iota((peers, rows), 1))[0] == iota((peers, rows), 0)).astype(F32)
    loads[2].wait()
    aligned[...] = dot(order[...], saved[...]).astype(BF16)
    loads[3].wait()

    def gather(turn, carry):
        wave = wave_at(turn)
        start = pl.multiple_of(wave * rows, 16)
        held = aligned[pl.ds(start, rows), :].astype(F32)
        pltpu.make_async_copy(
            scale_send.at[wave], scale_recv.at[wave], scale_recv_sem.at[wave]
        ).wait()
        all_scales = scale_recv[wave].reshape(peers, LANES).astype(BF16)
        scale = jnp.sum(jnp.where(ours, dot(holder, all_scales), 0.0), axis=1, keepdims=True)
        pltpu.make_async_copy(send.at[wave], recv.at[wave], recv_sem.at[wave]).wait()
        mixed = dot(together[...], recv[wave].reshape(MICRO * size, LANES)).astype(BF16)
        flat = jnp.concatenate(
            [mixed[j * rows : (j + 1) * rows] for j in range(groups)], axis=1
        )
        grad = dot(flat, weight[...], ((1,), (1,)))
        route_grad = jnp.sum(grad * held, axis=1, keepdims=True)
        sums = dot(holder_t, jnp.where(ours, route_grad, 0.0), precision=lax.Precision.HIGHEST)
        back_send[wave] = sums.reshape(peers, 1, LANES)

        def back(step, inner_carry):
            back_copy(wave, step).start()
            return inner_carry

        lax.fori_loop(others(wave), peers, back, 0)
        hidden[pl.ds(start, rows), :] = (scale * grad).astype(BF16)
        return carry

    lax.fori_loop(0, half, gather, 0)
    pltpu.make_async_copy(back_send.at[0, column], back_recv.at[me], back_recv_sem).start()
    placed[...] = dot(place[...], hidden[...]).astype(BF16)
    pltpu.make_async_copy(placed, hidden_hbm, store_sem).start()

    for m in range(MICRO):
        pipe_copy(m).wait_send()

    def left(wave, carry):
        pltpu.make_async_copy(send.at[wave], recv.at[wave], send_sem.at[wave]).wait()
        pltpu.make_async_copy(
            scale_send.at[wave], scale_recv.at[wave], scale_send_sem.at[wave]
        ).wait()
        return carry

    lax.fori_loop(1, half, left, 0)
    remote = pl.ds(0, peers - 1)
    both = pl.ds(0, MICRO)
    pltpu.make_async_copy(
        send.at[0, both, remote], recv.at[0, both, remote], send_sem.at[0]
    ).wait()
    pltpu.make_async_copy(
        scale_send.at[0, remote], scale_recv.at[0, remote], scale_send_sem.at[0]
    ).wait()
    pltpu.make_async_copy(back_recv, back_recv, back_recv_sem).wait()
    returned = back_recv[...].reshape(experts, LANES)
    slot_grad = [
        jnp.sum(
            slot[k] * dot(returned, named[k], ((0,), (0,)), lax.Precision.HIGHEST),
            axis=0,
            keepdims=True,
        )
        for k in range(TOP)
    ]
    mean = weights[0] * slot_grad[0] + weights[1] * slot_grad[1]
    logit = sum(named[k] * (weights[k] * (slot_grad[k] - mean)) for k in range(TOP))
    logit_ref[...] = logit
    away = pl.ds(0, experts - 1)
    pltpu.make_async_copy(back_recv.at[away], back_recv.at[away], back_send_sem).wait()
    pltpu.make_async_copy(placed, hidden_hbm, store_sem).wait()


def finish(hidden_hbm, logit_hbm, router_hbm, out_hbm, grad_in_hbm, hidden, logit, router, grad_in, sem):
    loads = [
        pltpu.make_async_copy(source, target, sem.at[at])
        for at, (source, target) in enumerate(
            ((hidden_hbm, hidden), (logit_hbm, logit), (router_hbm, router))
        )
    ]
    for load in loads:
        load.start()
    loads[0].wait()
    stores = [
        pltpu.make_async_copy(hidden, out_hbm.at[0], sem.at[3]),
        pltpu.make_async_copy(grad_in, grad_in_hbm.at[0], sem.at[4]),
    ]
    stores[0].start()
    loads[1].wait()
    by_token = logit[...].T
    high = by_token.astype(BF16)
    low = (by_token - high.astype(F32)).astype(BF16)
    loads[2].wait()
    grad_in[...] = (dot(high, router[...]) + dot(low, router[...])).astype(BF16)
    stores[1].start()
    for store in stores:
        store.wait()


def solution(mesh):
    experts = mesh.shape["expert"]

    def on_device(grad_sent, routes, router_probs, saved_hidden, w_down, w_router):
        model_width = grad_sent.shape[2]
        slots, width = saved_hidden.shape[1:]
        tokens = routes.shape[1] // MICRO
        depth = model_width // LANES
        columns = experts // depth
        half = depth // 2
        peers = 2 * columns
        unit = model_width // LANES * CAP
        in_vmem = pl.BlockSpec(memory_space=pltpu.VMEM)
        in_place = pl.BlockSpec(memory_space=pl.ANY)
        hidden, logit = pl.pallas_call(
            functools.partial(kernel, columns, depth),
            out_shape=(
                jax.ShapeDtypeStruct((slots, width), BF16),
                jax.ShapeDtypeStruct((experts, MICRO * tokens), F32),
            ),
            in_specs=[in_place] * 5,
            out_specs=(in_place, in_vmem),
            scratch_shapes=[
                pltpu.VMEM((TOP, MICRO * tokens), jnp.int32),
                pltpu.VMEM((experts, MICRO * tokens), F32),
                pltpu.VMEM((MICRO, tokens, model_width), BF16),
                pltpu.VMEM((MICRO, half, peers * CAP, tokens), BF16),
                pltpu.VMEM((slots, slots), BF16),
                pltpu.VMEM((slots, slots), BF16),
                pltpu.VMEM((peers * unit, peers * unit), BF16),
                pltpu.VMEM((MICRO * peers * unit, MICRO * peers * unit), BF16),
                pltpu.VMEM((half, MICRO, peers, unit, LANES), BF16),
                pltpu.VMEM((half, MICRO, peers, unit, LANES), BF16),
                pltpu.VMEM((slots, width), BF16),
                pltpu.VMEM((slots, width), BF16),
                pltpu.VMEM((width, model_width), BF16),
                pltpu.VMEM((half, peers, 1, LANES), F32),
                pltpu.VMEM((half, peers, 1, LANES), F32),
                pltpu.VMEM((slots, width), BF16),
                pltpu.VMEM((slots, width), BF16),
                pltpu.VMEM((half, peers, 1, LANES), F32),
                pltpu.VMEM((experts, 1, LANES), F32),
                pltpu.SemaphoreType.DMA((4,)),
                pltpu.SemaphoreType.DMA,
                pltpu.SemaphoreType.DMA((MICRO,)),
                pltpu.SemaphoreType.DMA((MICRO,)),
                pltpu.SemaphoreType.DMA((half,)),
                pltpu.SemaphoreType.DMA((half,)),
                pltpu.SemaphoreType.DMA((half,)),
                pltpu.SemaphoreType.DMA((half,)),
                pltpu.SemaphoreType.DMA,
                pltpu.SemaphoreType.DMA,
                pltpu.SemaphoreType.REGULAR,
                pltpu.SemaphoreType.REGULAR((depth.bit_length() - 1,)),
            ],
            compiler_params=pltpu.CompilerParams(
                collective_id=0, has_side_effects=True, vmem_limit_bytes=67043328
            ),
            name="routed_backward",
        )(routes[0].T, router_probs[0].T, grad_sent, saved_hidden, w_down)
        return pl.pallas_call(
            finish,
            out_shape=(
                jax.ShapeDtypeStruct((1, slots, width), BF16),
                jax.ShapeDtypeStruct((1, MICRO * tokens, model_width), BF16),
            ),
            in_specs=[in_place] * 3,
            out_specs=(in_place, in_place),
            scratch_shapes=[
                pltpu.VMEM((slots, width), BF16),
                pltpu.VMEM((experts, MICRO * tokens), F32),
                pltpu.VMEM((experts, model_width), BF16),
                pltpu.VMEM((MICRO * tokens, model_width), BF16),
                pltpu.SemaphoreType.DMA((5,)),
            ],
            compiler_params=pltpu.CompilerParams(vmem_limit_bytes=67043328),
            name="finish",
        )(hidden, logit, w_router.T)

    placed = (
        P("pipe", "expert", None),
        P("pipe", "expert", None),
        P("pipe", "expert", None),
        P("pipe", "expert", None),
        P("expert", None, None),
        P(),
    )
    return jax.shard_map(
        on_device,
        mesh=mesh,
        in_specs=placed,
        out_specs=(P("pipe", "expert", None), P("pipe", "expert", None)),
        check_vma=False,
    )
```

time: 112 us -> 110 us (0.982)
  the two profiles are of different devices: /device:TPU:24 before, /device:TPU:1 now
where the time goes in v4:
time: 110 us; the launch traced here: 108 us
  Pallas kernels  107 us (97%)
    pallas_call x1, Pallas kernels, on_device(): pl.pallas_call(functools.partial(kernel, columns, depth), out_shape=(jax....  105 us
    pallas_call x1, Pallas kernels, on_device(): pl.pallas_call(finish, out_shape=(jax.ShapeDtypeStruct((1, slots, width),...  2.42 us

profile of v4, /device:TPU:1, one launch (start us, length us, event | category | flops | bytes accessed | tf_op | source)
XLA Modules:
  0.0 108.1 jit_solution(4285887028596330217)
XLA Ops:
  0.6 105.0 %routed_backward.1 = (bf16[384,768]{1,0:T(8,128)(2,1)}, f32[64,128]{1,0:T(8,128)}) custom-call(s32[2,128]{1,0:T(2,128)} %bitcast.9, f32[64,128]{1,0:T(8,128)} %bitcast.8, bf16[1,128,2048]{2,1,0:T(8,128)(2,1)} %grad_hbm.1, bf16[1,384,768]{2,1,0:T(8,128)(2,1)} %saved_hbm.1, bf16[1,768,2048]{2,1,0:T(8,128)(2,1)} %weight_hbm.1), custom_call_target="tpu_custom_call" | custom-call | tf_op jit(solution)/shard_map/routed_backward/pallas_call | solution.py:431
  105.6 2.4 %finish.1 = (bf16[1,384,768]{2,1,0:T(8,128)(2,1)}, bf16[1,128,2048]{2,1,0:T(8,128)(2,1)}) custom-call(bf16[384,768]{1,0:T(8,128)(2,1)} %get-tuple-element.4.hidden_hbm, f32[64,128]{1,0:T(8,128)} %get-tuple-element.5.logit_hbm, bf16[64,2048]{1,0:T(8,128)(2,1)} %bitcast.7), custom_call_target="tpu_custom_call" | custom-call | tf_op jit(solution)/shard_map/finish/pallas_call | solution.py:477

commit v5 on v4

--- a/solution.py
+++ b/solution.py
@@ -300,12 +300,9 @@
 
     order[...] = onehot(iota((slots, slots), 1) == natural(iota((slots, 1), 0)))
     place[...] = onehot(iota((slots, slots), 0) == natural(iota((1, slots), 1)))
-    j, inner = split(iota((MICRO * size, 1), 0), rows)
-    m, inner = split(inner, peers * CAP)
+    j, inner = split(iota((size, 1), 0), peers * CAP)
     p, own = split(inner, CAP)
-    together[...] = onehot(
-        iota((MICRO * size, MICRO * size), 1) == m * size + p * unit + j * CAP + own
-    )
+    together[...] = onehot(iota((size, size), 1) == p * unit + j * CAP + own)
 
     def peer_and_slot(line):
         m, inner = split(line, peers * CAP)
@@ -329,10 +326,12 @@
         all_scales = scale_recv[wave].reshape(peers, LANES).astype(BF16)
         scale = jnp.sum(jnp.where(ours, dot(holder, all_scales), 0.0), axis=1, keepdims=True)
         pltpu.make_async_copy(send.at[wave], recv.at[wave], recv_sem.at[wave]).wait()
-        mixed = dot(together[...], recv[wave].reshape(MICRO * size, LANES)).astype(BF16)
-        flat = jnp.concatenate(
-            [mixed[j * rows : (j + 1) * rows] for j in range(groups)], axis=1
-        )
+        parts = []
+        for m in range(MICRO):
+            mixed = dot(together[...], recv[wave, m].reshape(size, LANES))
+            pieces = [mixed[j * peers * CAP : (j + 1) * peers * CAP] for j in range(groups)]
+            parts.append(jnp.concatenate(pieces, axis=1))
+        flat = jnp.concatenate(parts, axis=0).astype(BF16)
         grad = dot(flat, weight[...], ((1,), (1,)))
         route_grad = jnp.sum(grad * held, axis=1, keepdims=True)
         sums = dot(holder_t, jnp.where(ours, route_grad, 0.0), precision=lax.Precision.HIGHEST)
@@ -444,7 +443,7 @@
                 pltpu.VMEM((slots, slots), BF16),
                 pltpu.VMEM((slots, slots), BF16),
                 pltpu.VMEM((peers * unit, peers * unit), BF16),
-                pltpu.VMEM((MICRO * peers * unit, MICRO * peers * unit), BF16),
+                pltpu.VMEM((peers * unit, peers * unit), BF16),
                 pltpu.VMEM((half, MICRO, peers, unit, LANES), BF16),
                 pltpu.VMEM((half, MICRO, peers, unit, LANES), BF16),
                 pltpu.VMEM((slots, width), BF16),

time: 110 us -> 109 us (level)
  no operation moved by 1% of the time
where the time goes in v5:
time: 109 us; the launch traced here: 108 us
  Pallas kernels  107 us (98%)
    pallas_call x1, Pallas kernels, on_device(): pl.pallas_call(functools.partial(kernel, columns, depth), out_shape=(jax....  105 us
    pallas_call x1, Pallas kernels, on_device(): pl.pallas_call(finish, out_shape=(jax.ShapeDtypeStruct((1, slots, width),...  2.42 us

profile of v5, /device:TPU:1, one launch (start us, length us, event | category | flops | bytes accessed | tf_op | source)
XLA Modules:
  0.0 107.7 jit_solution(5252105938637570213)
XLA Ops:
  0.6 104.6 %routed_backward.1 = (bf16[384,768]{1,0:T(8,128)(2,1)}, f32[64,128]{1,0:T(8,128)}) custom-call(s32[2,128]{1,0:T(2,128)} %bitcast.9, f32[64,128]{1,0:T(8,128)} %bitcast.8, bf16[1,128,2048]{2,1,0:T(8,128)(2,1)} %grad_hbm.1, bf16[1,384,768]{2,1,0:T(8,128)(2,1)} %saved_hbm.1, bf16[1,768,2048]{2,1,0:T(8,128)(2,1)} %weight_hbm.1), custom_call_target="tpu_custom_call" | custom-call | tf_op jit(solution)/shard_map/routed_backward/pallas_call | solution.py:430
  105.3 2.4 %finish.1 = (bf16[1,384,768]{2,1,0:T(8,128)(2,1)}, bf16[1,128,2048]{2,1,0:T(8,128)(2,1)}) custom-call(bf16[384,768]{1,0:T(8,128)(2,1)} %get-tuple-element.4.hidden_hbm, f32[64,128]{1,0:T(8,128)} %get-tuple-element.5.logit_hbm, bf16[64,2048]{1,0:T(8,128)(2,1)} %bitcast.7), custom_call_target="tpu_custom_call" | custom-call | tf_op jit(solution)/shard_map/finish/pallas_call | solution.py:476
